TPU v7x, 32 devices: a whole 2x2x4 slice. The times are simulated.
32 devices in a mesh: blk: 4 (over y, x), hid: 8 (over z, core).
Axes of the slice: x: 2, y: 2, z: 4, core: 2. Of those that a mesh axis runs over, the one named last changes fastest.
Arguments:
- images: bfloat16 [8192, 1024], P(('blk', 'hid')), may hold values from -0.1875 to 0.1875
- caption_ids: int32 [8192], P(('blk', 'hid')), may hold values from 0 to 2047, as said below
- captions: bfloat16 [2048, 1024], P(('blk', 'hid')), may hold values from -0.75 to 0.75
- caption_feats: bfloat16 [2048, 1024], P(('blk', 'hid')), may hold values from -1.5 to 1.5
- w_in: bfloat16 [1024, 32768], P('blk', 'hid'), may hold values from -0.1875 to 0.1875
- w_out: bfloat16 [1024, 32768], P('blk', 'hid'), may hold values from -0.03125 to 0.03125
- logit_scale: float32 [1], replicated, may hold values from 8 to 16
- logit_bias: float32 [1], replicated, may hold values from -3 to -1
Outputs:
- image_grad: bfloat16 [8192, 1024], P(('blk', 'hid'))
- feat_grad: bfloat16 [2048, 1024], P(('blk', 'hid'))
- w_in_grad: bfloat16 [1024, 32768], P('blk', 'hid')
- w_out_grad: bfloat16 [1024, 32768], P('blk', 'hid')
Inputs may be any that keep to these rules, and one draw needn't show every extreme that they name: `caption_ids`: the image rows of block b name caption rows of the caption blocks b, b - 1, ..., b - 2 (mod the number of blocks); the first image row of every block names the last caption row of its own block, the second names the first.
All inputs are finite; a program needn't handle non-finite values.
Results may differ from a plain program's by a relative error of at most 0.019.
Values may be sent and summed in bfloat16 or wider, within the bound.
A program may use at most 128 MiB of HBM per device.

v0:
```python
import math

import jax
import jax.numpy as jnp
from jax import lax
from jax.sharding import PartitionSpec as P

HOPS = 2


def from_behind(shard, axis, by):
    length = lax.axis_size(axis)
    return lax.ppermute(shard, axis, [(i, (i + by) % length) for i in range(length)])


def gelu_parts(values):
    coefficient = math.sqrt(2.0 / math.pi)
    inner_arg = coefficient * (values + 0.044715 * values * values * values)
    tangent = jnp.tanh(inner_arg)
    output = 0.5 * values * (1.0 + tangent)
    gelu_slope = 0.5 * (1.0 + tangent) + 0.5 * values * (1.0 - tangent * tangent) * coefficient * (
        1.0 + 3.0 * 0.044715 * values * values
    )
    return (output, gelu_slope)


def contract(left_side, right_side, left_dim, right_dim):
    return lax.dot_general(
        left_side,
        right_side,
        (((left_dim,), (right_dim,)), ((), ())),
        preferred_element_type=jnp.float32,
    )


def shards(images, caption_ids, captions, caption_feats, w_in, w_out, logit_scale, logit_bias):
    temper = logit_scale[0]
    offset = logit_bias[0]
    cap_rows = captions.shape[0]
    devices = lax.axis_size(("blk", "hid"))
    device = lax.axis_index(("blk", "hid"))
    cap_local = lax.broadcasted_iota(jnp.int32, (cap_rows, 1), 0)
    image_acc = jnp.zeros(images.shape, jnp.float32)
    current = captions
    carried = None
    own_grad = None
    for stride in range(HOPS + 1):
        if stride > 0:
            current = from_behind(current, ("blk", "hid"), 1)
        holder = (device - stride) % devices
        global_rows = holder * cap_rows + cap_local
        positive = (global_rows == caption_ids[None, :]).astype(jnp.float32)
        logits = temper * contract(current, images, 1, 1) + offset
        pair_grad = (jax.nn.sigmoid(logits) - positive).astype(jnp.bfloat16)
        image_acc = image_acc + contract(pair_grad, current, 0, 0)
        hop_term = temper * jnp.dot(pair_grad, images, preferred_element_type=jnp.float32)
        if stride > 0:
            carried = (
                from_behind(carried.astype(jnp.bfloat16), ("blk", "hid"), 1).astype(carried.dtype)
                + hop_term
            )
        else:
            carried = hop_term
    own_grad = from_behind(carried.astype(jnp.bfloat16), ("blk", "hid"), -HOPS).astype(
        carried.dtype
    )
    image_grad = (temper * image_acc).astype(jnp.bfloat16)
    caption_round = own_grad.astype(jnp.bfloat16)
    rows_all, feats_all = (
        lax.all_gather(caption_round, "hid", axis=0, tiled=True),
        lax.all_gather(caption_feats, "hid", axis=0, tiled=True),
    )
    hidden = w_in.shape[1]
    full_in, full_out = (
        lax.all_gather(w_in, "blk", axis=0, tiled=True),
        lax.all_gather(w_out, "blk", axis=0, tiled=True),
    )
    pre_act = jnp.dot(feats_all, full_in, preferred_element_type=jnp.float32)
    act_grad = jnp.dot(rows_all, full_out, preferred_element_type=jnp.float32)
    output, gelu_slope = gelu_parts(pre_act)
    active = output.astype(jnp.bfloat16)
    pre_grad = (act_grad * gelu_slope).astype(jnp.bfloat16)
    summed = lax.psum_scatter(
        jnp.concatenate(
            [contract(feats_all, pre_grad, 0, 0), contract(rows_all, active, 0, 0)], axis=1
        ).astype(jnp.bfloat16),
        "blk",
        scatter_dimension=0,
        tiled=True,
    ).astype(jnp.float32)
    w_in_grad = summed[:, :hidden].astype(jnp.bfloat16)
    w_out_grad = summed[:, hidden:].astype(jnp.bfloat16)
    branch = lax.psum_scatter(
        contract(pre_grad, full_in, 1, 1).astype(jnp.bfloat16),
        "hid",
        scatter_dimension=0,
        tiled=True,
    ).astype(jnp.float32)
    feat_grad = (own_grad + branch).astype(jnp.bfloat16)
    return (image_grad, feat_grad, w_in_grad, w_out_grad)


def solution(mesh):
    return jax.shard_map(
        shards,
        mesh=mesh,
        in_specs=(
            P(("blk", "hid"), None),
            P(("blk", "hid")),
            P(("blk", "hid"), None),
            P(("blk", "hid"), None),
            P("blk", "hid"),
            P("blk", "hid"),
            P(),
            P(),
        ),
        out_specs=(
            P(("blk", "hid"), None),
            P(("blk", "hid"), None),
            P("blk", "hid"),
            P("blk", "hid"),
        ),
        check_vma=False,
    )
```

profile of v0, /device:TPU:0, one launch (start us, length us, event | category | flops | bytes accessed | tf_op | source)
XLA Modules:
  0.0 465.0 jit_solution(1923815996936304609)
XLA Ops:
  7.2 0.0 copy-start
  7.2 0.0 all-gather.9.cloned.1.call-start
  7.2 0.7 all-gather.9.cloned.1.call-update
  7.9 0.0 all-gather.11.cloned.1.call-start
  8.0 0.7 all-gather.11.cloned.1.call-update
  8.7 0.0 all-gather.5.cloned.1.call-start
  8.7 0.5 collective-permute-start
  10.6 0.0 copy-done
  10.6 1.2 fusion.32
  11.8 0.2 fusion.13
  12.0 2.7 collective-permute-start.2
  14.7 3.3 collective-permute-done
  18.0 0.0 collective-permute-start.1
  18.0 1.0 fusion.33
  19.0 1.6 collective-permute-done.2
  20.6 0.2 add_convert_fusion.2
  20.9 0.1 collective-permute-start.3
  20.9 5.3 %collective-permute-done.1 = bf16[64,1024]{1,0:T(8,128)(2,1)S(1)} collective-permute-done((bf16[64,1024]{1,0:T(8,128)(2,1)S(1)}, bf16[64,1024]{1,0:T(8,128)(2,1)S(1)}, u32[]{:S(2)}, u32[]{:S(2)}) %collective-permute-start.1) | collective-permute-done | bytes 131104 | tf_op jit(solution)/shard_map/ppermute | solution.py:13
  26.2 1.0 fusion.34
  27.2 0.2 convolution_multiply_fusion
  27.4 4.3 collective-permute-done.3
  31.7 0.1 collective-permute-start.4
  31.8 5.6 %collective-permute-done.4 = bf16[64,1024]{1,0:T(8,128)(2,1)S(1)} collective-permute-done((bf16[64,1024]{1,0:T(8,128)(2,1)S(1)}, bf16[64,1024]{1,0:T(8,128)(2,1)S(1)}, u32[]{:S(2)}, u32[]{:S(2)}) %collective-permute-start.4) | collective-permute-done | bytes 131104 | tf_op jit(solution)/shard_map/ppermute | solution.py:13
  37.4 0.0 copy-start.2
  37.4 0.7 copy-done.2
  38.1 0.0 all-gather.5.cloned.1.call-update
  38.1 0.0 all-gather.7.cloned.1.call-start
  38.1 0.5 all-gather.7.cloned.1.call-update
  38.7 0.0 reduce-scatter.3.cloned.1.call-start
  38.7 0.0 all-gather.9.cloned.1.call-done
  38.8 88.0 %all-gather.11.cloned.1.call-done = bf16[1024,4096]{1,0:T(8,128)(2,1)} async-done(((bf16[256,4096]{1,0:T(8,128)(2,1)}), bf16[1024,4096]{1,0:T(8,128)(2,1)}) %all-gather.11.cloned.1.call-update) | async-done | bytes 8388624 | tf_op jit(solution)/shard_map/all_gather | solution.py:75
  126.8 11.5 %fusion.41 = f32[512,4096]{1,0:T(8,128)} fusion(bf16[512,1024]{1,0:T(8,128)(2,1)} %all-gather.9.cloned.1.call-done, bf16[1024,4096]{1,0:T(8,128)(2,1)} %all-gather.11.cloned.1.call-done), kind=kOutput, calls=%fused_computation.62 | convolution fusion | flops 4294967296 | bytes 17825792 | tf_op jit(solution)/shard_map/dot_general | solution.py:78
  138.2 13.0 %all-gather.5.cloned.1.call-done = bf16[512,1024]{1,0:T(8,128)(2,1)} async-done(((bf16[64,1024]{1,0:T(8,128)(2,1)}), bf16[512,1024]{1,0:T(8,128)(2,1)}) %all-gather.5.cloned.1.call-update) | async-done | bytes 1048592 | tf_op jit(solution)/shard_map/all_gather | solution.py:70
  151.2 88.8 %all-gather.7.cloned.1.call-done = bf16[1024,4096]{1,0:T(8,128)(2,1)} async-done(((bf16[256,4096]{1,0:T(8,128)(2,1)}), bf16[1024,4096]{1,0:T(8,128)(2,1)}) %all-gather.7.cloned.1.call-update) | async-done | bytes 8388624 | tf_op jit(solution)/shard_map/all_gather | solution.py:76
  240.0 0.0 copy-start.5
  240.0 12.2 %fusion.6 = bf16[512,4096]{1,0:T(8,128)(2,1)S(1)} fusion(f32[512,4096]{1,0:T(8,128)} %fusion.41, bf16[512,1024]{1,0:T(8,128)(2,1)} %all-gather.5.cloned.1.call-done, bf16[1024,4096]{1,0:T(8,128)(2,1)} %all-gather.7.cloned.1.call-done), kind=kOutput, calls=%fused_computation.9 | convolution fusion | flops 4334813184 | bytes 22020096 | tf_op jit(solution)/shard_map/dot_general | solution.py:79
  252.2 0.0 copy-start.8
  252.2 1.9 copy-done.8
  254.2 0.0 copy-done.5
  254.2 0.0 copy-start.6
  254.2 5.5 %convolution_convert_fusion.1 = bf16[512,1024]{1,0:T(8,128)(2,1)} fusion(bf16[512,4096]{1,0:T(8,128)(2,1)S(1)} %fusion.6, bf16[1024,4096]{1,0:T(8,128)(2,1)S(1)} %copy-done.5), kind=kOutput, calls=%fused_computation.17 | convolution fusion | flops 4295491584 | bytes 13631488 | tf_op jit(solution)/shard_map/dot_general | solution.py:28
  259.7 0.0 reduce-scatter.3.cloned.1.call-update
  259.7 0.0 copy-start.7
  259.7 0.2 reduce-scatter.5.cloned.1.call-start
  260.0 0.0 copy-done.6
  260.0 7.0 %convert_bitcast_fusion = bf16[1024,4096]{0,1:T(8,128)(2,1)S(1)} fusion(bf16[512,4096]{1,0:T(8,128)(2,1)} %copy-done.8, bf16[512,1024]{1,0:T(8,128)(2,1)S(1)} %copy-done.6), kind=kOutput, calls=%fused_computation.11 | convolution fusion | flops 4299161600 | bytes 13631488 | tf_op jit(solution)/shard_map/dot_general | solution.py:28
  267.0 0.0 copy-done.7
  267.0 8.0 %convolution_convert_fusion = bf16[1024,4096]{0,1:T(8,128)(2,1)S(1)} fusion(bf16[512,1024]{1,0:T(8,128)(2,1)S(1)} %copy-done.7, f32[512,4096]{1,0:T(8,128)} %fusion.41), kind=kOutput, calls=%fused_computation.12 | convolution fusion | flops 4318035968 | bytes 17825792 | tf_op jit(solution)/shard_map/dot_general | solution.py:28
  275.0 8.7 %pad_maximum_fusion = bf16[1024,8192]{0,1:T(8,128)(2,1)} fusion(bf16[1024,4096]{0,1:T(8,128)(2,1)S(1)} %convolution_convert_fusion, bf16[1024,4096]{0,1:T(8,128)(2,1)S(1)} %convert_bitcast_fusion), kind=kLoop, calls=%fused_computation | loop fusion | flops 33554432 | bytes 33554432 | tf_op jit(solution)/shard_map/concatenate | solution.py:84
  283.7 0.0 copy-start.4
  283.7 0.0 copy-start.3
  283.7 0.0 reduce-scatter.5.cloned.1.call-update
  283.8 0.9 copy-done.4
  284.6 0.3 fusion.40
  284.9 0.3 convolution_add_fusion.1
  285.3 1.1 fusion.12
  286.4 6.5 %reduce-scatter.3.cloned.1.call-done = bf16[64,1024]{1,0:T(8,128)(2,1)} async-done(((bf16[512,1024]{1,0:T(8,128)(2,1)}), bf16[64,1024]{1,0:T(8,128)(2,1)}) %reduce-scatter.3.cloned.1.call-update) | async-done | bytes 131088 | tf_op jit(solution)/shard_map/reduce_scatter | solution.py:93
  292.9 0.0 copy-done.3
  292.9 1.7 add_convert_fusion
  294.5 152.9 %reduce-scatter.5.cloned.1.call-done = bf16[256,8192]{0,1:T(8,128)(2,1)} async-done(((bf16[1024,8192]{0,1:T(8,128)(2,1)}), bf16[256,8192]{0,1:T(8,128)(2,1)}) %reduce-scatter.5.cloned.1.call-update) | async-done | bytes 4194320 | tf_op jit(solution)/shard_map/reduce_scatter | solution.py:83
  447.4 3.8 fusion.39
  451.2 4.1 copy.14
  455.3 2.8 copy.13
  458.1 0.0 copy-done.1
  (5 shorter events, 0.0 us)
Async XLA Ops:
  7.2 3.4 copy-start
  7.2 31.6 %all-gather.9.cloned.1.call-start = ((), (), s32[]{:S(2)}) async-start(), calls=%async_computation.4 | async-start | bytes 1179648 | tf_op jit(solution)/shard_map/all_gather | solution.py:71
  7.9 118.8 %all-gather.11.cloned.1.call-start = ((), (), s32[]{:S(2)}) async-start(), calls=%async_computation.5 | async-start | bytes 10485760 | tf_op jit(solution)/shard_map/all_gather | solution.py:75
  8.7 142.5 %all-gather.5.cloned.1.call-start = ((), (), s32[]{:S(2)}) async-start(), calls=%async_computation.2 | async-start | bytes 1179648 | tf_op jit(solution)/shard_map/all_gather | solution.py:70
  8.7 9.3 %collective-permute-start = (bf16[64,1024]{1,0:T(8,128)(2,1)}, bf16[64,1024]{1,0:T(8,128)(2,1)S(1)}, u32[]{:S(2)}, u32[]{:S(2)}) collective-permute-start(bf16[64,1024]{1,0:T(8,128)(2,1)} %param.10), channel_id=1, source_target_pairs={{0,1},{1,2},{2,3},{3,4},{4,5},{5,6},{6,7},{7,8},{8,9},{9,10},{10,1... | collective-permute-start | bytes 393224 | tf_op jit(solution)/shard_map/ppermute | solution.py:13
  12.0 8.6 %collective-permute-start.2 = (bf16[64,1024]{1,0:T(8,128)(2,1)S(1)}, bf16[64,1024]{1,0:T(8,128)(2,1)S(1)}, u32[]{:S(2)}, u32[]{:S(2)}) collective-permute-start(bf16[64,1024]{1,0:T(8,128)(2,1)S(1)} %fusion.13), channel_id=1, source_target_pairs={{0,1},{1,2},{2,3},{3,4},{4,5},{5,6},{6,7},{7,8},{8,9},{9,10},{10,1... | collective-permute-start | bytes 393224 | tf_op jit(solution)/shard_map/ppermute | solution.py:13
  18.0 8.2 %collective-permute-start.1 = (bf16[64,1024]{1,0:T(8,128)(2,1)S(1)}, bf16[64,1024]{1,0:T(8,128)(2,1)S(1)}, u32[]{:S(2)}, u32[]{:S(2)}) collective-permute-start(bf16[64,1024]{1,0:T(8,128)(2,1)S(1)} %collective-permute-done), channel_id=1, source_target_pairs={{0,1},{1,2},{2,3},{3,4},{4,5},{5,6},{6,7},{7,8},{8,9},{9,10},{10,1... | collective-permute-start | bytes 393224 | tf_op jit(solution)/shard_map/ppermute | solution.py:13
  20.9 10.8 %collective-permute-start.3 = (bf16[64,1024]{1,0:T(8,128)(2,1)S(1)}, bf16[64,1024]{1,0:T(8,128)(2,1)S(1)}, u32[]{:S(2)}, u32[]{:S(2)}) collective-permute-start(bf16[64,1024]{1,0:T(8,128)(2,1)S(1)} %add_convert_fusion.2), channel_id=1, source_target_pairs={{0,1},{1,2},{2,3},{3,4},{4,5},{5,6},{6,7},{7,8},{8,9},{9,10},{10,1... | collective-permute-start | bytes 393224 | tf_op jit(solution)/shard_map/ppermute | solution.py:13
  31.7 5.7 %collective-permute-start.4 = (bf16[64,1024]{1,0:T(8,128)(2,1)S(1)}, bf16[64,1024]{1,0:T(8,128)(2,1)S(1)}, u32[]{:S(2)}, u32[]{:S(2)}) collective-permute-start(bf16[64,1024]{1,0:T(8,128)(2,1)S(1)} %add_convert_fusion.1), channel_id=1, source_target_pairs={{0,30},{1,31},{2,0},{3,1},{4,2},{5,3},{6,4},{7,5},{8,6},{9,7},{10,... | collective-permute-start | bytes 393224 | tf_op jit(solution)/shard_map/ppermute | solution.py:13
  37.4 0.7 copy-start.2
  38.1 201.9 %all-gather.7.cloned.1.call-start = ((), (), s32[]{:S(2)}) async-start(), calls=%async_computation.3 | async-start | bytes 10485760 | tf_op jit(solution)/shard_map/all_gather | solution.py:76
  38.7 254.2 %reduce-scatter.3.cloned.1.call-start = ((), (), s32[]{:S(2)}) async-start(), calls=%async_computation.6 | async-start | bytes 1179648 | tf_op jit(solution)/shard_map/reduce_scatter | solution.py:93
  240.0 14.2 %copy-start.5 = (bf16[1024,4096]{1,0:T(8,128)(2,1)S(1)}, bf16[1024,4096]{1,0:T(8,128)(2,1)}, u32[]{:S(2)}) copy-start(bf16[1024,4096]{1,0:T(8,128)(2,1)} %all-gather.11.cloned.1.call-done) | copy-start | bytes 25165828
  252.2 1.9 copy-start.8
  254.2 5.8 %copy-start.6 = (bf16[512,1024]{1,0:T(8,128)(2,1)S(1)}, bf16[512,1024]{1,0:T(8,128)(2,1)}, u32[]{:S(2)}) copy-start(bf16[512,1024]{1,0:T(8,128)(2,1)} %all-gather.9.cloned.1.call-done) | copy-start | bytes 3145732
  259.7 7.3 %copy-start.7 = (bf16[512,1024]{1,0:T(8,128)(2,1)S(1)}, bf16[512,1024]{1,0:T(8,128)(2,1)}, u32[]{:S(2)}) copy-start(bf16[512,1024]{1,0:T(8,128)(2,1)} %all-gather.5.cloned.1.call-done) | copy-start | bytes 3145732
  259.7 187.7 %reduce-scatter.5.cloned.1.call-start = ((), (), s32[]{:S(2)}) async-start(), calls=%async_computation.7 | async-start | bytes 20971520 | tf_op jit(solution)/shard_map/reduce_scatter | solution.py:83
  283.7 0.9 copy-start.4
  283.7 9.1 %copy-start.3 = (bf16[64,1024]{1,0:T(8,128)(2,1)S(1)}, bf16[64,1024]{1,0:T(8,128)(2,1)}, u32[]{:S(2)}) copy-start(bf16[64,1024]{1,0:T(8,128)(2,1)} %copy-done.2) | copy-start | bytes 393220
  292.9 165.3 %copy-start.1 = (bf16[256,1024]{1,0:T(8,128)(2,1)S(1)}, bf16[256,1024]{1,0:T(8,128)(2,1)}, u32[]{:S(2)}) copy-start(bf16[256,1024]{1,0:T(8,128)(2,1)} %param.8) | copy-start | bytes 1572868
Sparse Core Ops, SparseCore 0:
  9.6 29.1 all-gather.8
  40.6 86.1 all-gather.10
  128.9 22.2 all-gather.4
  152.9 87.0 all-gather.6
  259.8 32.9 reduce-scatter.2
  295.8 151.5 reduce-scatter.4
where the time goes:
time: 465 us
  waiting for transfers between devices  371 us (80%)
  matrix products  49.8 us (11%)
  between operations  15.6 us (3%)
  local copies, waits for them, and re-layouts  14.2 us (3%)
  other arithmetic  10.4 us (2%)
    reduce_scatter x1, waiting for transfers between devices, shards(): lax.psum_scatter(jnp.concatenate([contract(feats_all, pre_grad, 0, 0), co...  153 us
    all_gather x1, waiting for transfers between devices, shards(): lax.all_gather(w_out, 'blk', axis=0, tiled=True)  88.8 us
    all_gather x1, waiting for transfers between devices, shards(): lax.all_gather(w_in, 'blk', axis=0, tiled=True)  88 us
    dot_general x9, matrix products, contract(): lax.dot_general(left_side, right_side, (((left_dim,), (right_dim,)), ((),...  25.5 us
    ppermute x5, waiting for transfers between devices, from_behind(): lax.ppermute(shard, axis, [(i, (i + by) % length) for i in range(length)])  20.1 us
    all_gather x1, waiting for transfers between devices, shards(): lax.all_gather(caption_round, 'hid', axis=0, tiled=True)  13 us
    dot_general x1, matrix products, shards(): act_grad = jnp.dot(rows_all, full_out, preferred_element_type=jnp.float32)  12.2 us
    dot_general x1, matrix products, shards(): pre_act = jnp.dot(feats_all, full_in, preferred_element_type=jnp.float32)  11.5 us
  transfers between devices with their start and end apart: 11, of which 10 were waited for; matrix products, arithmetic and copies ran while one was open for 9% of the time, Pallas kernels for 0%

commit v1 on v0

--- a/solution.py
+++ b/solution.py
@@ -66,36 +66,26 @@
     )
     image_grad = (temper * image_acc).astype(jnp.bfloat16)
     caption_round = own_grad.astype(jnp.bfloat16)
-    rows_all, feats_all = (
-        lax.all_gather(caption_round, "hid", axis=0, tiled=True),
-        lax.all_gather(caption_feats, "hid", axis=0, tiled=True),
-    )
-    hidden = w_in.shape[1]
-    full_in, full_out = (
-        lax.all_gather(w_in, "blk", axis=0, tiled=True),
-        lax.all_gather(w_out, "blk", axis=0, tiled=True),
-    )
+    both = ("blk", "hid")
+    feats_all = lax.all_gather(caption_feats, both, axis=0, tiled=True)
+    full_in = lax.all_to_all(w_in, "blk", 1, 0, tiled=True)
+    full_out = lax.all_to_all(w_out, "blk", 1, 0, tiled=True)
+    rows_all = lax.all_gather(caption_round, both, axis=0, tiled=True)
     pre_act = jnp.dot(feats_all, full_in, preferred_element_type=jnp.float32)
     act_grad = jnp.dot(rows_all, full_out, preferred_element_type=jnp.float32)
     output, gelu_slope = gelu_parts(pre_act)
     active = output.astype(jnp.bfloat16)
     pre_grad = (act_grad * gelu_slope).astype(jnp.bfloat16)
-    summed = lax.psum_scatter(
-        jnp.concatenate(
-            [contract(feats_all, pre_grad, 0, 0), contract(rows_all, active, 0, 0)], axis=1
-        ).astype(jnp.bfloat16),
-        "blk",
-        scatter_dimension=0,
-        tiled=True,
-    ).astype(jnp.float32)
-    w_in_grad = summed[:, :hidden].astype(jnp.bfloat16)
-    w_out_grad = summed[:, hidden:].astype(jnp.bfloat16)
-    branch = lax.psum_scatter(
-        contract(pre_grad, full_in, 1, 1).astype(jnp.bfloat16),
-        "hid",
-        scatter_dimension=0,
-        tiled=True,
-    ).astype(jnp.float32)
+    part = contract(pre_grad, full_in, 1, 1).astype(jnp.bfloat16)
+    part = lax.psum_scatter(part, "blk", scatter_dimension=0, tiled=True)
+    part = lax.psum_scatter(part, "hid", scatter_dimension=0, tiled=True)
+    branch = part.astype(jnp.float32)
+    w_in_grad = lax.all_to_all(
+        contract(feats_all, pre_grad, 0, 0).astype(jnp.bfloat16), "blk", 0, 1, tiled=True
+    )
+    w_out_grad = lax.all_to_all(
+        contract(rows_all, active, 0, 0).astype(jnp.bfloat16), "blk", 0, 1, tiled=True
+    )
     feat_grad = (own_grad + branch).astype(jnp.bfloat16)
     return (image_grad, feat_grad, w_in_grad, w_out_grad)
 

time: 465 us -> 309 us (0.66)
  waiting for transfers between devices: 371 us -> 197 us
  starting transfers between devices: 3.81 us -> 21 us
  other arithmetic: 10.4 us -> 1.63 us
  local copies, waits for them, and re-layouts: 14.2 us -> 20.3 us
    all_gather x4 -> x2, waiting for transfers between devices: 190 us -> 52.2 us  [the longest x1 52.2 us: shards(): rows_all = lax.all_gather(caption_round, both, axis=0, tiled=True)]
    reduce_scatter x2, waiting for transfers between devices: 159 us -> 59.6 us  [the longest x1 59.6 us: shards(): part = lax.psum_scatter(part, 'blk', scatter_dimension=0, tiled=True)]
    all_to_all x0 -> x4, waiting for transfers between devices: none -> 67.6 us  [the longest x1 24.1 us: shards(): full_out = lax.all_to_all(w_out, 'blk', 1, 0, tiled=True)]
    all_to_all x0 -> x4, starting transfers between devices: none -> 17.5 us  [the longest x1 4.77 us: shards(): full_in = lax.all_to_all(w_in, 'blk', 1, 0, tiled=True)]
    all_to_all x0 -> x4, local copies, waits for them, and re-layouts: none -> 11.1 us  [the longest x1 4.04 us: shards(): full_out = lax.all_to_all(w_out, 'blk', 1, 0, tiled=True)]
    concatenate x1 -> x0, other arithmetic: 8.74 us -> none  [shards(): jnp.concatenate([contract(feats_all, pre_grad, 0, 0), contract(rows_all,...]
    dot_general x9, matrix products: 25.5 us -> 31.3 us  [contract(): lax.dot_general(left_side, right_side, (((left_dim,), (right_dim,)), ((),...]
    unnamed x20 -> x16, local copies, waits for them, and re-layouts: 10.4 us -> 9.13 us
  transfers between devices with their start and end apart: 11 -> 13, of which waited for: 10 -> 10; matrix products, arithmetic and copies ran while one was open for 9% -> 17% of each run, Pallas kernels for 0% -> 0%
where the time goes in v1:
time: 309 us; the launch traced here: 308 us
  waiting for transfers between devices  197 us (64%)
  matrix products  52.8 us (17%)
  starting transfers between devices  21 us (7%)
  local copies, waits for them, and re-layouts  20.3 us (7%)
  between operations  15.2 us (5%)
    reduce_scatter x1, waiting for transfers between devices, shards(): part = lax.psum_scatter(part, 'blk', scatter_dimension=0, tiled=True)  59.6 us
    all_gather x1, waiting for transfers between devices, shards(): rows_all = lax.all_gather(caption_round, both, axis=0, tiled=True)  52.2 us
    dot_general x9, matrix products, contract(): lax.dot_general(left_side, right_side, (((left_dim,), (right_dim,)), ((),...  31.3 us
    all_to_all x1, waiting for transfers between devices, shards(): full_out = lax.all_to_all(w_out, 'blk', 1, 0, tiled=True)  24.1 us
    all_to_all x1, waiting for transfers between devices, shards(): full_in = lax.all_to_all(w_in, 'blk', 1, 0, tiled=True)  21.8 us
    all_to_all x1, waiting for transfers between devices, shards(): lax.all_to_all(contract(feats_all, pre_grad, 0, 0).astype(jnp.bfloat16),...  21.7 us
    ppermute x5, waiting for transfers between devices, from_behind(): lax.ppermute(shard, axis, [(i, (i + by) % length) for i in range(length)])  17 us
    dot_general x1, matrix products, shards(): act_grad = jnp.dot(rows_all, full_out, preferred_element_type=jnp.float32)  11.9 us
  transfers between devices with their start and end apart: 13, of which 10 were waited for; matrix products, arithmetic and copies ran while one was open for 17% of the time, Pallas kernels for 0%

profile of v1, /device:TPU:0, one launch (start us, length us, event | category | flops | bytes accessed | tf_op | source)
XLA Modules:
  0.0 308.2 jit_solution(6208078136115789033)
XLA Ops:
  7.2 0.0 copy-start
  7.2 0.0 copy-start.1
  7.2 0.0 all-gather.5.cloned.1.call-start
  7.2 0.7 all-gather.5.cloned.1.call-update
  7.9 0.0 all-gather.3.cloned.1.call-start
  8.0 0.5 collective-permute-start
  9.8 0.0 copy-done
  9.8 1.2 fusion.30
  11.1 0.2 fusion.11
  11.3 2.7 collective-permute-start.2
  14.0 3.3 %collective-permute-done = bf16[64,1024]{1,0:T(8,128)(2,1)S(1)} collective-permute-done((bf16[64,1024]{1,0:T(8,128)(2,1)}, bf16[64,1024]{1,0:T(8,128)(2,1)S(1)}, u32[]{:S(2)}, u32[]{:S(2)}) %collective-permute-start) | collective-permute-done | bytes 131104 | tf_op jit(solution)/shard_map/ppermute | solution.py:13
  17.3 0.0 collective-permute-start.1
  17.3 1.0 fusion.31
  18.3 1.6 collective-permute-done.2
  19.9 0.2 add_convert_fusion.2
  20.1 0.1 collective-permute-start.3
  20.2 5.1 %collective-permute-done.1 = bf16[64,1024]{1,0:T(8,128)(2,1)S(1)} collective-permute-done((bf16[64,1024]{1,0:T(8,128)(2,1)S(1)}, bf16[64,1024]{1,0:T(8,128)(2,1)S(1)}, u32[]{:S(2)}, u32[]{:S(2)}) %collective-permute-start.1) | collective-permute-done | bytes 131104 | tf_op jit(solution)/shard_map/ppermute | solution.py:13
  25.3 1.0 fusion.32
  26.3 0.2 convolution_multiply_fusion
  26.5 1.8 collective-permute-done.3
  28.3 0.1 collective-permute-start.4
  28.4 5.2 %collective-permute-done.4 = bf16[64,1024]{1,0:T(8,128)(2,1)S(1)} collective-permute-done((bf16[64,1024]{1,0:T(8,128)(2,1)S(1)}, bf16[64,1024]{1,0:T(8,128)(2,1)S(1)}, u32[]{:S(2)}, u32[]{:S(2)}) %collective-permute-start.4) | collective-permute-done | bytes 131104 | tf_op jit(solution)/shard_map/ppermute | solution.py:13
  33.6 0.0 copy-start.3
  33.6 0.7 copy-done.3
  34.3 0.0 all-gather.3.cloned.1.call-update
  34.3 0.0 copy-done.1
  34.3 2.5 copy.18
  36.8 4.8 %all-to-all-start.1 = ((bf16[256,4,1024]{0,2,1:T(8,128)(2,1)}), bf16[256,4,1024]{0,2,1:T(8,128)(2,1)S(1)}, u32[]{:S(2)}, u32[]{:S(2)}) async-start(bf16[256,4,1024]{0,2,1:T(8,128)(2,1)} %bitcast.58), calls=%async_computation.1 | async-start | bytes 4194304 | tf_op jit(solution)/shard_map/all_to_all | solution.py:71
  41.5 4.1 %copy.16 = bf16[256,4096]{0,1:T(8,128)(2,1)} copy(bf16[256,4096]{1,0:T(8,128)(2,1)} %param.13) | data formatting | bytes 4194304 | tf_op args[5]
  45.6 21.8 %all-to-all-done.1 = bf16[256,4,1024]{0,2,1:T(8,128)(2,1)S(1)} async-done(((bf16[256,4,1024]{0,2,1:T(8,128)(2,1)}), bf16[256,4,1024]{0,2,1:T(8,128)(2,1)S(1)}, u32[]{:S(2)}, u32[]{:S(2)}) %all-to-all-start.1) | async-done | bytes 2097184 | tf_op jit(solution)/shard_map/all_to_all | solution.py:71
  67.4 4.5 %all-to-all-start = ((bf16[256,4,1024]{0,2,1:T(8,128)(2,1)}), bf16[256,4,1024]{0,2,1:T(8,128)(2,1)}, u32[]{:S(2)}, u32[]{:S(2)}) async-start(bf16[256,4,1024]{0,2,1:T(8,128)(2,1)} %bitcast.57), calls=%async_computation | async-start | bytes 4194304 | tf_op jit(solution)/shard_map/all_to_all | solution.py:72
  71.9 0.0 reduce-scatter.3.cloned.1.call-start
  72.0 2.4 copy.19
  74.3 0.0 copy-start.2
  74.3 24.1 %all-to-all-done = bf16[256,4,1024]{0,2,1:T(8,128)(2,1)} async-done(((bf16[256,4,1024]{0,2,1:T(8,128)(2,1)}), bf16[256,4,1024]{0,2,1:T(8,128)(2,1)}, u32[]{:S(2)}, u32[]{:S(2)}) %all-to-all-start) | async-done | bytes 2097184 | tf_op jit(solution)/shard_map/all_to_all | solution.py:72
  98.5 4.0 %copy.17 = bf16[4,256,1024]{2,1,0:T(8,128)(2,1)} copy(bf16[4,256,1024]{1,2,0:T(8,128)(2,1)} %bitcast.3) | data formatting | bytes 4194304 | tf_op jit(solution)/shard_map/all_to_all | solution.py:72
  102.5 0.0 all-gather.5.cloned.1.call-done
  102.5 0.0 copy-done.2
  102.5 9.0 %fusion.38 = f32[2048,1024]{1,0:T(8,128)} fusion(bf16[2048,1024]{1,0:T(8,128)(2,1)} %all-gather.5.cloned.1.call-done, bf16[1024,1024]{1,0:T(8,128)(2,1)S(1)} %bitcast.63), kind=kOutput, calls=%fused_computation.57 | convolution fusion | flops 4294967296 | bytes 14680064 | tf_op jit(solution)/shard_map/dot_general | solution.py:74
  111.5 52.2 %all-gather.3.cloned.1.call-done = bf16[2048,1024]{1,0:T(8,128)(2,1)} async-done(((bf16[64,1024]{1,0:T(8,128)(2,1)}), bf16[2048,1024]{1,0:T(8,128)(2,1)}) %all-gather.3.cloned.1.call-update) | async-done | bytes 4194320 | tf_op jit(solution)/shard_map/all_gather | solution.py:73
  163.7 11.9 %fusion.6 = bf16[2048,1024]{1,0:T(8,128)(2,1)S(1)} fusion(f32[2048,1024]{1,0:T(8,128)} %fusion.38, bf16[2048,1024]{1,0:T(8,128)(2,1)} %all-gather.3.cloned.1.call-done, bf16[1024,1024]{1,0:T(8,128)(2,1)} %bitcast.65), kind=kOutput, calls=%fused_computation.8 | convolution fusion | flops 4334813184 | bytes 18874368 | tf_op jit(solution)/shard_map/dot_general | solution.py:75
  175.6 0.0 copy-start.6
  175.6 1.9 copy-done.6
  177.5 6.3 %convolution_convert_fusion = bf16[2048,1024]{1,0:T(8,128)(2,1)} fusion(bf16[2048,1024]{1,0:T(8,128)(2,1)S(1)} %fusion.6, bf16[1024,1024]{1,0:T(8,128)(2,1)S(1)} %bitcast.64), kind=kOutput, calls=%fused_computation.11 | convolution fusion | flops 4297064448 | bytes 10485760 | tf_op jit(solution)/shard_map/dot_general | solution.py:28
  183.8 0.0 reduce-scatter.3.cloned.1.call-update
  183.9 10.7 %fusion.8 = bf16[1024,1024]{1,0:T(8,128)(2,1)} fusion(bf16[2048,1024]{1,0:T(8,128)(2,1)} %all-gather.3.cloned.1.call-done, f32[2048,1024]{1,0:T(8,128)} %fusion.38), kind=kOutput, calls=%fused_computation.13 | convolution fusion | flops 4314890240 | bytes 14680064 | tf_op jit(solution)/shard_map/dot_general | solution.py:28
  194.6 3.6 %all-to-all-start.3 = ((bf16[4,256,1024]{2,1,0:T(8,128)(2,1)}), bf16[4,256,1024]{2,1,0:T(8,128)(2,1)S(1)}, u32[]{:S(2)}, u32[]{:S(2)}) async-start(bf16[4,256,1024]{2,1,0:T(8,128)(2,1)} %bitcast.61), calls=%async_computation.5 | async-start | bytes 4194304 | tf_op jit(solution)/shard_map/all_to_all | solution.py:86
  198.2 0.0 reduce-scatter.5.cloned.1.call-start
  198.3 59.6 %reduce-scatter.3.cloned.1.call-done = bf16[512,1024]{1,0:T(8,128)(2,1)} async-done(((bf16[2048,1024]{1,0:T(8,128)(2,1)}), bf16[512,1024]{1,0:T(8,128)(2,1)}) %reduce-scatter.3.cloned.1.call-update) | async-done | bytes 1048592 | tf_op jit(solution)/shard_map/reduce_scatter | solution.py:80
  257.9 0.0 reduce-scatter.5.cloned.1.call-update
  257.9 9.3 %convolution_convert_fusion.1 = bf16[1024,1024]{0,1:T(8,128)(2,1)} fusion(bf16[2048,1024]{1,0:T(8,128)(2,1)} %copy-done.6, bf16[2048,1024]{1,0:T(8,128)(2,1)} %all-gather.5.cloned.1.call-done), kind=kOutput, calls=%fused_computation.12 | convolution fusion | flops 4296015872 | bytes 10485760 | tf_op jit(solution)/shard_map/dot_general | solution.py:28
  267.2 0.0 copy-start.5
  267.2 0.0 all-to-all-done.3
  267.2 4.6 %all-to-all-start.2 = ((bf16[4,256,1024]{2,1,0:T(8,128)(2,1)}), bf16[4,256,1024]{2,1,0:T(8,128)(2,1)}, u32[]{:S(2)}, u32[]{:S(2)}) async-start(bf16[4,256,1024]{2,1,0:T(8,128)(2,1)} %bitcast.59), calls=%async_computation.4 | async-start | bytes 4194304 | tf_op jit(solution)/shard_map/all_to_all | solution.py:83
  271.8 0.0 copy-done.5
  271.9 0.3 fusion.37
  272.2 0.3 convolution_add_fusion.1
  272.5 1.1 fusion.10
  273.6 0.0 copy-start.4
  273.6 1.6 copy.23
  275.2 21.7 %all-to-all-done.2 = bf16[4,256,1024]{2,1,0:T(8,128)(2,1)} async-done(((bf16[4,256,1024]{2,1,0:T(8,128)(2,1)}), bf16[4,256,1024]{2,1,0:T(8,128)(2,1)}, u32[]{:S(2)}, u32[]{:S(2)}) %all-to-all-start.2) | async-done | bytes 2097184 | tf_op jit(solution)/shard_map/all_to_all | solution.py:83
  296.9 3.2 %copy.22 = bf16[4,32,8,1024]{3,2,0,1:T(8,128)(2,1)} copy(bf16[4,32,8,1024]{3,2,1,0:T(8,128)(2,1)} %bitcast.14) | data formatting | bytes 4194304 | tf_op jit(solution)/shard_map/all_to_all | solution.py:83
  300.0 0.0 copy-done.4
  300.1 1.6 add_convert_fusion
  (5 shorter events, 0.0 us)
Async XLA Ops:
  7.2 2.7 copy-start
  7.2 27.1 %copy-start.1 = (bf16[256,4096]{1,0:T(8,128)(2,1)S(1)}, bf16[256,4096]{1,0:T(8,128)(2,1)}, u32[]{:S(2)}) copy-start(bf16[256,4096]{1,0:T(8,128)(2,1)} %param.12) | copy-start | bytes 6291460
  7.2 95.3 %all-gather.5.cloned.1.call-start = ((), (), s32[]{:S(2)}) async-start(), calls=%async_computation.7 | async-start | bytes 4325376 | tf_op jit(solution)/shard_map/all_gather | solution.py:70
  7.9 155.8 %all-gather.3.cloned.1.call-start = ((), (), s32[]{:S(2)}) async-start(), calls=%async_computation.6 | async-start | bytes 4325376 | tf_op jit(solution)/shard_map/all_gather | solution.py:73
  8.0 9.3 %collective-permute-start = (bf16[64,1024]{1,0:T(8,128)(2,1)}, bf16[64,1024]{1,0:T(8,128)(2,1)S(1)}, u32[]{:S(2)}, u32[]{:S(2)}) collective-permute-start(bf16[64,1024]{1,0:T(8,128)(2,1)} %param.10), channel_id=1, source_target_pairs={{0,1},{1,2},{2,3},{3,4},{4,5},{5,6},{6,7},{7,8},{8,9},{9,10},{10,1... | collective-permute-start | bytes 393224 | tf_op jit(solution)/shard_map/ppermute | solution.py:13
  11.3 8.6 %collective-permute-start.2 = (bf16[64,1024]{1,0:T(8,128)(2,1)S(1)}, bf16[64,1024]{1,0:T(8,128)(2,1)S(1)}, u32[]{:S(2)}, u32[]{:S(2)}) collective-permute-start(bf16[64,1024]{1,0:T(8,128)(2,1)S(1)} %fusion.11), channel_id=1, source_target_pairs={{0,1},{1,2},{2,3},{3,4},{4,5},{5,6},{6,7},{7,8},{8,9},{9,10},{10,1... | collective-permute-start | bytes 393224 | tf_op jit(solution)/shard_map/ppermute | solution.py:13
  17.3 8.0 %collective-permute-start.1 = (bf16[64,1024]{1,0:T(8,128)(2,1)S(1)}, bf16[64,1024]{1,0:T(8,128)(2,1)S(1)}, u32[]{:S(2)}, u32[]{:S(2)}) collective-permute-start(bf16[64,1024]{1,0:T(8,128)(2,1)S(1)} %collective-permute-done), channel_id=1, source_target_pairs={{0,1},{1,2},{2,3},{3,4},{4,5},{5,6},{6,7},{7,8},{8,9},{9,10},{10,1... | collective-permute-start | bytes 393224 | tf_op jit(solution)/shard_map/ppermute | solution.py:13
  20.1 8.1 %collective-permute-start.3 = (bf16[64,1024]{1,0:T(8,128)(2,1)S(1)}, bf16[64,1024]{1,0:T(8,128)(2,1)S(1)}, u32[]{:S(2)}, u32[]{:S(2)}) collective-permute-start(bf16[64,1024]{1,0:T(8,128)(2,1)S(1)} %add_convert_fusion.2), channel_id=1, source_target_pairs={{0,1},{1,2},{2,3},{3,4},{4,5},{5,6},{6,7},{7,8},{8,9},{9,10},{10,1... | collective-permute-start | bytes 393224 | tf_op jit(solution)/shard_map/ppermute | solution.py:13
  28.3 5.3 %collective-permute-start.4 = (bf16[64,1024]{1,0:T(8,128)(2,1)S(1)}, bf16[64,1024]{1,0:T(8,128)(2,1)S(1)}, u32[]{:S(2)}, u32[]{:S(2)}) collective-permute-start(bf16[64,1024]{1,0:T(8,128)(2,1)S(1)} %add_convert_fusion.1), channel_id=1, source_target_pairs={{0,30},{1,31},{2,0},{3,1},{4,2},{5,3},{6,4},{7,5},{8,6},{9,7},{10,... | collective-permute-start | bytes 393224 | tf_op jit(solution)/shard_map/ppermute | solution.py:13
  33.6 0.7 copy-start.3
  36.8 30.6 %all-to-all-start.1 = ((bf16[256,4,1024]{0,2,1:T(8,128)(2,1)}), bf16[256,4,1024]{0,2,1:T(8,128)(2,1)S(1)}, u32[]{:S(2)}, u32[]{:S(2)}) async-start(bf16[256,4,1024]{0,2,1:T(8,128)(2,1)} %bitcast.58), calls=%async_computation.1 | async-start | bytes 4194304 | tf_op jit(solution)/shard_map/all_to_all | solution.py:71
  67.4 31.1 %all-to-all-start = ((bf16[256,4,1024]{0,2,1:T(8,128)(2,1)}), bf16[256,4,1024]{0,2,1:T(8,128)(2,1)}, u32[]{:S(2)}, u32[]{:S(2)}) async-start(bf16[256,4,1024]{0,2,1:T(8,128)(2,1)} %bitcast.57), calls=%async_computation | async-start | bytes 4194304 | tf_op jit(solution)/shard_map/all_to_all | solution.py:72
  71.9 186.0 %reduce-scatter.3.cloned.1.call-start = ((), (), s32[]{:S(2)}) async-start(), calls=%async_computation.8 | async-start | bytes 5242880 | tf_op jit(solution)/shard_map/reduce_scatter | solution.py:80
  74.3 28.2 %copy-start.2 = (bf16[4,256,1024]{2,1,0:T(8,128)(2,1)S(1)}, bf16[4,256,1024]{2,1,0:T(8,128)(2,1)}, u32[]{:S(2)}) copy-start(bf16[4,256,1024]{2,1,0:T(8,128)(2,1)} %copy.19) | copy-start | bytes 6291460
  175.6 1.9 copy-start.6
  194.6 72.7 %all-to-all-start.3 = ((bf16[4,256,1024]{2,1,0:T(8,128)(2,1)}), bf16[4,256,1024]{2,1,0:T(8,128)(2,1)S(1)}, u32[]{:S(2)}, u32[]{:S(2)}) async-start(bf16[4,256,1024]{2,1,0:T(8,128)(2,1)} %bitcast.61), calls=%async_computation.5 | async-start | bytes 4194304 | tf_op jit(solution)/shard_map/all_to_all | solution.py:86
  198.2 101.8 %reduce-scatter.5.cloned.1.call-start = ((), (), s32[]{:S(2)}) async-start(), calls=%async_computation.9 | async-start | bytes 1179648 | tf_op jit(solution)/shard_map/reduce_scatter | solution.py:81
  267.2 4.6 %copy-start.5 = (bf16[64,1024]{1,0:T(8,128)(2,1)S(1)}, bf16[64,1024]{1,0:T(8,128)(2,1)}, u32[]{:S(2)}) copy-start(bf16[64,1024]{1,0:T(8,128)(2,1)} %param.10) | copy-start | bytes 393220
  267.2 29.6 %all-to-all-start.2 = ((bf16[4,256,1024]{2,1,0:T(8,128)(2,1)}), bf16[4,256,1024]{2,1,0:T(8,128)(2,1)}, u32[]{:S(2)}, u32[]{:S(2)}) async-start(bf16[4,256,1024]{2,1,0:T(8,128)(2,1)} %bitcast.59), calls=%async_computation.4 | async-start | bytes 4194304 | tf_op jit(solution)/shard_map/all_to_all | solution.py:83
  273.6 26.4 %copy-start.4 = (bf16[64,1024]{1,0:T(8,128)(2,1)S(1)}, bf16[64,1024]{1,0:T(8,128)(2,1)}, u32[]{:S(2)}) copy-start(bf16[64,1024]{1,0:T(8,128)(2,1)} %copy-done.3) | copy-start | bytes 393220
Sparse Core Ops, SparseCore 0:
  11.0 89.1 all-gather.4
  103.8 59.8 all-gather.2
  184.0 73.8 reduce-scatter.2
  260.0 32.6 reduce-scatter.4

commit v2 on v1

--- a/solution.py
+++ b/solution.py
@@ -1,8 +1,11 @@
+import functools
 import math
 
 import jax
 import jax.numpy as jnp
 from jax import lax
+from jax.experimental import pallas as pl
+from jax.experimental.pallas import tpu as pltpu
 from jax.sharding import PartitionSpec as P
 
 HOPS = 2
@@ -31,6 +34,165 @@
         (((left_dim,), (right_dim,)), ((), ())),
         preferred_element_type=jnp.float32,
     )
+
+
+def spread_kernel(n_blk, n_hid, rows_ref, win_ref, wout_ref, all_ref, fin_ref, fout_ref,
+                  keep_in, keep_out, local_sem, w_send, w_recv,
+                  a_send, a_recv, b_send, b_recv, c_send, c_recv):
+    blk = lax.axis_index("blk")
+    hid = lax.axis_index("hid")
+    pairs = n_hid // 2
+    core = lax.rem(hid, 2)
+    place = lax.div(hid, 2)
+    cap = rows_ref.shape[0]
+    depth = win_ref.shape[0]
+    width = fin_ref.shape[1]
+    mesh_id = pl.DeviceIdType.MESH
+
+    def peer_blk(step):
+        return lax.rem(blk + step, n_blk)
+
+    def peer_place(step):
+        return lax.rem(place + step, pairs)
+
+    def rows_of(block, spot, side):
+        start = ((block * pairs + spot) * 2 + side) * cap
+        return pl.ds(pl.multiple_of(start, cap), cap)
+
+    partner = (blk, place * 2 + 1 - core)
+    barrier = pltpu.get_barrier_semaphore()
+    for step in range(1, n_blk):
+        pl.semaphore_signal(barrier, inc=1, device_id=(peer_blk(step), hid), device_id_type=mesh_id)
+    for step in range(1, pairs):
+        pl.semaphore_signal(
+            barrier, inc=1, device_id=(blk, peer_place(step) * 2 + core), device_id_type=mesh_id
+        )
+    pl.semaphore_signal(barrier, inc=1, device_id=partner, device_id_type=mesh_id)
+    pl.semaphore_wait(barrier, n_blk + pairs - 1)
+
+    started = []
+
+    def send(src, dst, send_sem, recv_sem, device):
+        copy = pltpu.make_async_remote_copy(
+            src_ref=src, dst_ref=dst, send_sem=send_sem, recv_sem=recv_sem,
+            device_id=device, device_id_type=mesh_id,
+        )
+        copy.start()
+        started.append(copy)
+        return copy
+
+    own = rows_of(blk, place, core)
+    along = []
+    for step in range(1, pairs):
+        along.append(send(rows_ref, all_ref.at[own], a_send.at[step - 1], a_recv.at[step - 1],
+                          (blk, peer_place(step) * 2 + core)))
+    across = {}
+    for step in range(1, n_blk):
+        across[(step, 0)] = send(rows_ref, all_ref.at[own], b_send.at[step - 1, 0],
+                                 b_recv.at[step - 1, 0], (peer_blk(step), hid))
+    twin = [send(rows_ref, all_ref.at[own], c_send.at[0, 0], c_recv.at[0, 0], partner)]
+    locals_ = [pltpu.make_async_copy(rows_ref, all_ref.at[own], local_sem.at[0])]
+    mine = pl.ds(pl.multiple_of(blk * width, width), width)
+    takes = [
+        pltpu.make_async_copy(win_ref.at[:, mine], keep_in, local_sem.at[1]),
+        pltpu.make_async_copy(wout_ref.at[:, mine], keep_out, local_sem.at[2]),
+    ]
+    for copy in locals_ + takes:
+        copy.start()
+    band = pl.ds(pl.multiple_of(blk * depth, depth), depth)
+    weights = []
+
+    def send_weight(which, src_ref, dst_ref):
+        for step in range(1, n_blk):
+            other = pl.ds(pl.multiple_of(peer_blk(step) * width, width), width)
+            weights.append(send(src_ref.at[:, other], dst_ref.at[band, :],
+                                w_send.at[which, step - 1], w_recv.at[which, step - 1],
+                                (peer_blk(step), hid)))
+
+    for step in range(1, pairs):
+        along[step - 1].wait_recv()
+        got = rows_of(blk, lax.rem(place + pairs - step, pairs), core)
+        for far in range(1, n_blk):
+            across[(far, step)] = send(all_ref.at[got], all_ref.at[got], b_send.at[far - 1, step],
+                                       b_recv.at[far - 1, step], (peer_blk(far), hid))
+        twin.append(send(all_ref.at[got], all_ref.at[got], c_send.at[0, step],
+                         c_recv.at[0, step], partner))
+    send_weight(0, win_ref, fin_ref)
+    send_weight(1, wout_ref, fout_ref)
+    puts = [
+        pltpu.make_async_copy(keep_in, fin_ref.at[band, :], local_sem.at[3]),
+        pltpu.make_async_copy(keep_out, fout_ref.at[band, :], local_sem.at[4]),
+    ]
+    for take, put in zip(takes, puts):
+        take.wait()
+        put.start()
+    for step in range(pairs):
+        spot = lax.rem(place + pairs - step, pairs)
+        for far in range(1, n_blk):
+            across[(far, step)].wait_recv()
+            got = rows_of(lax.rem(blk + n_blk - far, n_blk), spot, core)
+            twin.append(send(all_ref.at[got], all_ref.at[got], c_send.at[far, step],
+                             c_recv.at[far, step], partner))
+    for copy in weights + twin:
+        copy.wait_recv()
+    for copy in started:
+        copy.wait_send()
+    for copy in locals_ + puts:
+        copy.wait()
+
+
+def spread(rows, w_in, w_out):
+    n_blk, n_hid = lax.axis_size("blk"), lax.axis_size("hid")
+    depth, hidden = w_in.shape
+    width = hidden // n_blk
+    pairs = n_hid // 2
+    dma = pltpu.SemaphoreType.DMA
+    near = max(pairs - 1, 1)
+    full = jax.ShapeDtypeStruct((depth * n_blk, width), w_in.dtype)
+    return pl.pallas_call(
+        functools.partial(spread_kernel, n_blk, n_hid),
+        out_shape=(
+            jax.ShapeDtypeStruct((rows.shape[0] * n_blk * n_hid, rows.shape[1]), rows.dtype),
+            full,
+            full,
+        ),
+        in_specs=[
+            pl.BlockSpec(memory_space=pltpu.VMEM),
+            pl.BlockSpec(memory_space=pl.ANY),
+            pl.BlockSpec(memory_space=pl.ANY),
+        ],
+        out_specs=[pl.BlockSpec(memory_space=pl.ANY)] * 3,
+        scratch_shapes=[
+            pltpu.VMEM((depth, width), w_in.dtype),
+            pltpu.VMEM((depth, width), w_in.dtype),
+            dma((5,)),
+            dma((2, n_blk - 1)), dma((2, n_blk - 1)),
+            dma((near,)), dma((near,)),
+            dma((n_blk - 1, pairs)), dma((n_blk - 1, pairs)),
+            dma((n_blk, pairs)), dma((n_blk, pairs)),
+        ],
+        compiler_params=pltpu.CompilerParams(collective_id=0, has_side_effects=True),
+    )(rows, w_in, w_out)
+
+
+def fold_rows(part):
+    n_blk, n_hid = lax.axis_size("blk"), lax.axis_size("hid")
+    pairs = n_hid // 2
+    hid = lax.axis_index("hid")
+    core, place = hid % 2, hid // 2
+    parts = part.reshape(n_blk, pairs, 2, -1, part.shape[1])
+    give = lax.dynamic_index_in_dim(parts, 1 - core, 2, keepdims=False)
+    keep = lax.dynamic_index_in_dim(parts, core, 2, keepdims=False)
+    came = lax.ppermute(give, "hid", [(i, i ^ 1) for i in range(n_hid)])
+    both = (keep.astype(jnp.float32) + came.astype(jnp.float32)).astype(part.dtype)
+    spread_out = lax.all_to_all(both, "blk", 0, 0, tiled=True)
+    mine = jnp.sum(spread_out.astype(jnp.float32), axis=0).astype(part.dtype)
+    total = lax.dynamic_index_in_dim(mine, place, 0, keepdims=False).astype(jnp.float32)
+    for step in range(1, pairs):
+        piece = lax.dynamic_index_in_dim(mine, (place + step) % pairs, 0, keepdims=False)
+        moves = [(i, (i + 2 * step) % n_hid) for i in range(n_hid)]
+        total = total + lax.ppermute(piece, "hid", moves).astype(jnp.float32)
+    return total
 
 
 def shards(images, caption_ids, captions, caption_feats, w_in, w_out, logit_scale, logit_bias):
@@ -68,18 +230,14 @@
     caption_round = own_grad.astype(jnp.bfloat16)
     both = ("blk", "hid")
     feats_all = lax.all_gather(caption_feats, both, axis=0, tiled=True)
-    full_in = lax.all_to_all(w_in, "blk", 1, 0, tiled=True)
-    full_out = lax.all_to_all(w_out, "blk", 1, 0, tiled=True)
-    rows_all = lax.all_gather(caption_round, both, axis=0, tiled=True)
+    rows_all, full_in, full_out = spread(caption_round, w_in, w_out)
     pre_act = jnp.dot(feats_all, full_in, preferred_element_type=jnp.float32)
     act_grad = jnp.dot(rows_all, full_out, preferred_element_type=jnp.float32)
     output, gelu_slope = gelu_parts(pre_act)
     active = output.astype(jnp.bfloat16)
     pre_grad = (act_grad * gelu_slope).astype(jnp.bfloat16)
     part = contract(pre_grad, full_in, 1, 1).astype(jnp.bfloat16)
-    part = lax.psum_scatter(part, "blk", scatter_dimension=0, tiled=True)
-    part = lax.psum_scatter(part, "hid", scatter_dimension=0, tiled=True)
-    branch = part.astype(jnp.float32)
+    branch = fold_rows(part)
     w_in_grad = lax.all_to_all(
         contract(feats_all, pre_grad, 0, 0).astype(jnp.bfloat16), "blk", 0, 1, tiled=True
     )

time: 309 us -> 250 us (0.81)
  waiting for transfers between devices: 197 us -> 66.7 us
  Pallas kernels: 0 us -> 86.6 us
  local copies, waits for them, and re-layouts: 20.3 us -> 7.9 us
  matrix products: 52.8 us -> 43.9 us
  other arithmetic: 1.63 us -> 8.41 us
    pallas_call x0 -> x1, Pallas kernels: none -> 86.6 us  [spread(): pl.pallas_call(functools.partial(spread_kernel, n_blk, n_hid), out_shape=...]
    reduce_scatter x2 -> x0, waiting for transfers between devices: 59.6 us -> none  [the longest x1 59.6 us: shards(): part = lax.psum_scatter(part, 'blk', scatter_dimension=0, tiled=True)]
    all_gather x1 -> x0, waiting for transfers between devices: 52.2 us -> none  [shards(): rows_all = lax.all_gather(caption_round, both, axis=0, tiled=True)]
    all_to_all x2 -> x1, waiting for transfers between devices: 45.9 us -> 15.7 us  [fold_rows(): spread_out = lax.all_to_all(both, 'blk', 0, 0, tiled=True)]
    all_to_all x1, waiting for transfers between devices: 0.01 us -> 21 us  [shards(): lax.all_to_all(contract(rows_all, active, 0, 0).astype(jnp.bfloat16), 'bl...]
    all_to_all x1, waiting for transfers between devices: 21.7 us -> 12.2 us  [shards(): lax.all_to_all(contract(feats_all, pre_grad, 0, 0).astype(jnp.bfloat16),...]
    unnamed x16 -> x18, local copies, waits for them, and re-layouts: 9.13 us -> 0.69 us
    all_to_all x2 -> x0, local copies, waits for them, and re-layouts: 6.42 us -> none  [the longest x1 4.04 us: shards(): full_out = lax.all_to_all(w_out, 'blk', 1, 0, tiled=True)]
  transfers between devices with their start and end apart: 13 -> 13, of which waited for: 10 -> 8; matrix products, arithmetic and copies ran while one was open for 17% -> 14% of each run, Pallas kernels for 0% -> 35%
where the time goes in v2:
time: 250 us; the launch traced here: 249 us
  Pallas kernels  86.6 us (35%)
  waiting for transfers between devices  66.7 us (27%)
  matrix products  43.9 us (18%)
  starting transfers between devices  20 us (8%)
  between operations  15.7 us (6%)
  other arithmetic  8.41 us (3%)
  local copies, waits for them, and re-layouts  7.9 us (3%)
    pallas_call x1, Pallas kernels, spread(): pl.pallas_call(functools.partial(spread_kernel, n_blk, n_hid), out_shape=...  86.6 us
    dot_general x9, matrix products, contract(): lax.dot_general(left_side, right_side, (((left_dim,), (right_dim,)), ((),...  27.4 us
    all_to_all x1, waiting for transfers between devices, shards(): lax.all_to_all(contract(rows_all, active, 0, 0).astype(jnp.bfloat16), 'bl...  21 us
    ppermute x5, waiting for transfers between devices, from_behind(): lax.ppermute(shard, axis, [(i, (i + by) % length) for i in range(length)])  17.1 us
    all_to_all x1, waiting for transfers between devices, fold_rows(): spread_out = lax.all_to_all(both, 'blk', 0, 0, tiled=True)  15.7 us
    all_to_all x1, waiting for transfers between devices, shards(): lax.all_to_all(contract(feats_all, pre_grad, 0, 0).astype(jnp.bfloat16),...  12.2 us
    dot_general x1, matrix products, shards(): act_grad = jnp.dot(rows_all, full_out, preferred_element_type=jnp.float32)  8.78 us
    dot_general x1, matrix products, shards(): pre_act = jnp.dot(feats_all, full_in, preferred_element_type=jnp.float32)  7.06 us
  transfers between devices with their start and end apart: 13, of which 8 were waited for; matrix products, arithmetic and copies ran while one was open for 14% of the time, Pallas kernels for 35%

profile of v2, /device:TPU:0, one launch (start us, length us, event | category | flops | bytes accessed | tf_op | source)
XLA Modules:
  0.0 249.3 jit_solution(6144200240732129442)
XLA Ops:
  7.2 0.0 copy-start
  7.2 0.0 all-gather.2.cloned.1.call-start
  7.2 0.7 all-gather.2.cloned.1.call-update
  7.9 0.5 collective-permute-start
  9.8 0.0 copy-done
  9.8 1.2 fusion.31
  11.0 0.2 fusion.12
  11.2 2.7 %collective-permute-start.2 = (bf16[64,1024]{1,0:T(8,128)(2,1)S(1)}, bf16[64,1024]{1,0:T(8,128)(2,1)S(1)}, u32[]{:S(2)}, u32[]{:S(2)}) collective-permute-start(bf16[64,1024]{1,0:T(8,128)(2,1)S(1)} %fusion.12), channel_id=1, source_target_pairs={{0,1},{1,2},{2,3},{3,4},{4,5},{5,6},{6,7},{7,8},{8,9},{9,10},{10,1... | collective-permute-start | bytes 393224 | tf_op jit(solution)/shard_map/ppermute | solution.py:16
  14.0 3.3 %collective-permute-done = bf16[64,1024]{1,0:T(8,128)(2,1)S(1)} collective-permute-done((bf16[64,1024]{1,0:T(8,128)(2,1)}, bf16[64,1024]{1,0:T(8,128)(2,1)S(1)}, u32[]{:S(2)}, u32[]{:S(2)}) %collective-permute-start) | collective-permute-done | bytes 131104 | tf_op jit(solution)/shard_map/ppermute | solution.py:16
  17.2 0.0 collective-permute-start.1
  17.2 1.0 fusion.32
  18.2 1.6 collective-permute-done.2
  19.9 0.2 add_convert_fusion.1
  20.1 0.1 collective-permute-start.3
  20.1 5.1 %collective-permute-done.1 = bf16[64,1024]{1,0:T(8,128)(2,1)S(1)} collective-permute-done((bf16[64,1024]{1,0:T(8,128)(2,1)S(1)}, bf16[64,1024]{1,0:T(8,128)(2,1)S(1)}, u32[]{:S(2)}, u32[]{:S(2)}) %collective-permute-start.1) | collective-permute-done | bytes 131104 | tf_op jit(solution)/shard_map/ppermute | solution.py:16
  25.2 1.0 fusion.33
  26.2 0.2 convolution_multiply_fusion
  26.4 1.8 collective-permute-done.3
  28.3 0.1 collective-permute-start.4
  28.3 5.3 %collective-permute-done.4.rows_ref = bf16[64,1024]{1,0:T(8,128)(2,1)S(1)} collective-permute-done((bf16[64,1024]{1,0:T(8,128)(2,1)S(1)}, bf16[64,1024]{1,0:T(8,128)(2,1)S(1)}, u32[]{:S(2)}, u32[]{:S(2)}) %collective-permute-start.4) | collective-permute-done | bytes 131104 | tf_op jit(solution)/shard_map/ppermute | solution.py:16
  33.7 0.7 copy-done.2
  34.3 86.6 %shard_map.111 = (bf16[2048,1024]{1,0:T(8,128)(2,1)}, bf16[1024,1024]{1,0:T(8,128)(2,1)}, bf16[1024,1024]{1,0:T(8,128)(2,1)}) custom-call(bf16[64,1024]{1,0:T(8,128)(2,1)} %copy-done.2, bf16[256,4096]{1,0:T(8,128)(2,1)} %win_ref.1, bf16[256,4096]{1,0:T(8,128)(2,1)} %wout_ref.1), custom_call_target="tpu_custom_call" | custom-call | tf_op jit(solution)/shard_map/pallas_call | solution.py:152
  121.0 0.0 all-gather.2.cloned.1.call-done
  121.0 0.0 copy-start.5
  121.0 0.0 copy-start.7
  121.0 7.1 %fusion.43 = f32[1024,2048]{0,1:T(8,128)S(1)} fusion(bf16[2048,1024]{1,0:T(8,128)(2,1)} %all-gather.2.cloned.1.call-done, bf16[1024,1024]{1,0:T(8,128)(2,1)} %get-tuple-element.9), kind=kOutput, calls=%fused_computation.68 | convolution fusion | flops 4294967296 | bytes 14680064 | tf_op jit(solution)/shard_map/dot_general | solution.py:234
  128.1 0.0 copy-done.5
  128.1 0.0 copy-done.7
  128.1 0.0 copy-start.6
  128.1 8.8 %fusion.6 = bf16[2048,1024]{1,0:T(8,128)(2,1)S(1)} fusion(f32[1024,2048]{0,1:T(8,128)S(1)} %fusion.43, bf16[2048,1024]{1,0:T(8,128)(2,1)S(1)} %copy-done.5, bf16[1024,1024]{1,0:T(8,128)(2,1)S(1)} %copy-done.7), kind=kOutput, calls=%fused_computation.8 | convolution fusion | flops 4334813184 | bytes 18874368 | tf_op jit(solution)/shard_map/dot_general | solution.py:235
  136.9 0.0 copy-done.6
  136.9 0.0 copy-start.8
  136.9 5.0 %convolution_convert_fusion = bf16[2048,1024]{1,0:T(8,128)(2,1)S(1)} fusion(bf16[2048,1024]{1,0:T(8,128)(2,1)S(1)} %fusion.6, bf16[1024,1024]{1,0:T(8,128)(2,1)S(1)} %copy-done.6), kind=kOutput, calls=%fused_computation.14 | convolution fusion | flops 4297064448 | bytes 10485760 | tf_op jit(solution)/shard_map/dot_general | solution.py:31
  141.9 0.0 copy-done.8
  141.9 0.0 copy-start.1
  141.9 1.7 dynamic-slice_bitcast_fusion
  143.7 0.0 collective-permute-start.5
  143.7 6.0 %fusion.9 = bf16[1024,1024]{1,0:T(8,128)(2,1)} fusion(bf16[2048,1024]{1,0:T(8,128)(2,1)S(1)} %copy-done.5, f32[1024,2048]{0,1:T(8,128)S(1)} %fusion.43), kind=kOutput, calls=%fused_computation.17 | convolution fusion | flops 4314890240 | bytes 14680064 | tf_op jit(solution)/shard_map/dot_general | solution.py:31
  149.6 0.0 copy-done.1
  149.6 3.8 %all-to-all-start.2 = ((bf16[4,256,1024]{2,1,0:T(8,128)(2,1)}), bf16[4,256,1024]{2,1,0:T(8,128)(2,1)S(1)}, u32[]{:S(2)}, u32[]{:S(2)}) async-start(bf16[4,256,1024]{2,1,0:T(8,128)(2,1)} %bitcast.85), calls=%async_computation.2 | async-start | bytes 4194304 | tf_op jit(solution)/shard_map/all_to_all | solution.py:244
  153.4 0.0 collective-permute-done.5
  153.4 4.6 %fusion.7 = bf16[4,4,64,1024]{3,2,1,0:T(8,128)(2,1)} fusion(bf16[4,4,64,1024]{3,2,1,0:T(8,128)(2,1)} %collective-permute-done.5, bf16[4,4,2,64,1024]{4,3,2,1,0:T(8,128)(2,1)} %bitcast.81, s32[]{:T(128)S(6)} %select_n.59), kind=kLoop, calls=%fused_computation.12 | loop fusion | flops 4194304 | bytes 6291460 | tf_op jit(solution)/shard_map/convert_element_type | solution.py:187
  158.0 21.0 %all-to-all-done.2 = bf16[4,256,1024]{2,1,0:T(8,128)(2,1)S(1)} async-done(((bf16[4,256,1024]{2,1,0:T(8,128)(2,1)}), bf16[4,256,1024]{2,1,0:T(8,128)(2,1)S(1)}, u32[]{:S(2)}, u32[]{:S(2)}) %all-to-all-start.2) | async-done | bytes 2097184 | tf_op jit(solution)/shard_map/all_to_all | solution.py:244
  179.0 4.5 %all-to-all-start = ((bf16[4,4,64,1024]{3,2,1,0:T(8,128)(2,1)}), bf16[4,4,64,1024]{3,2,1,0:T(8,128)(2,1)}, u32[]{:S(2)}, u32[]{:S(2)}) async-start(bf16[4,4,64,1024]{3,2,1,0:T(8,128)(2,1)} %fusion.7), calls=%async_computation | async-start | bytes 4194304 | tf_op jit(solution)/shard_map/all_to_all | solution.py:188
  183.5 9.3 %convolution_convert_fusion.1 = bf16[1024,1024]{0,1:T(8,128)(2,1)} fusion(bf16[2048,1024]{1,0:T(8,128)(2,1)} %copy-done.8, bf16[2048,1024]{1,0:T(8,128)(2,1)} %all-gather.2.cloned.1.call-done), kind=kOutput, calls=%fused_computation.16 | convolution fusion | flops 4296015872 | bytes 10485760 | tf_op jit(solution)/shard_map/dot_general | solution.py:31
  192.9 15.7 %all-to-all-done = bf16[4,4,64,1024]{3,2,1,0:T(8,128)(2,1)} async-done(((bf16[4,4,64,1024]{3,2,1,0:T(8,128)(2,1)}), bf16[4,4,64,1024]{3,2,1,0:T(8,128)(2,1)}, u32[]{:S(2)}, u32[]{:S(2)}) %all-to-all-start) | async-done | bytes 2097184 | tf_op jit(solution)/shard_map/all_to_all | solution.py:188
  208.6 4.5 %all-to-all-start.1 = ((bf16[4,256,1024]{2,1,0:T(8,128)(2,1)}), bf16[4,256,1024]{2,1,0:T(8,128)(2,1)}, u32[]{:S(2)}, u32[]{:S(2)}) async-start(bf16[4,256,1024]{2,1,0:T(8,128)(2,1)} %bitcast.82), calls=%async_computation.1 | async-start | bytes 4194304 | tf_op jit(solution)/shard_map/all_to_all | solution.py:241
  213.1 0.0 copy-done.4
  213.1 0.3 fusion.42
  213.4 1.3 convolution_add_fusion.1
  214.7 2.0 reduce_sum.12
  216.7 0.8 dynamic-slice_bitcast_fusion.3
  217.5 0.6 collective-permute-start.6
  218.1 3.3 %collective-permute-start.8 = (bf16[64,1024]{1,0:T(8,128)(2,1)}, bf16[64,1024]{1,0:T(8,128)(2,1)}, u32[]{:S(2)}, u32[]{:S(2)}) collective-permute-start(bf16[64,1024]{1,0:T(8,128)(2,1)} %get-tuple-element.11), channel_id=1, source_target_pairs={{0,6},{1,7},{2,0},{3,1},{4,2},{5,3},{6,4},{7,5},{8,14},{9,15},{10,... | collective-permute-start | bytes 393224 | tf_op jit(solution)/shard_map/ppermute | solution.py:194
  221.3 0.0 collective-permute-start.7
  221.3 2.3 fusion.11
  223.7 1.6 copy.17
  225.3 12.2 %all-to-all-done.1 = bf16[4,256,1024]{2,1,0:T(8,128)(2,1)} async-done(((bf16[4,256,1024]{2,1,0:T(8,128)(2,1)}), bf16[4,256,1024]{2,1,0:T(8,128)(2,1)}, u32[]{:S(2)}, u32[]{:S(2)}) %all-to-all-start.1) | async-done | bytes 2097184 | tf_op jit(solution)/shard_map/all_to_all | solution.py:241
  237.5 3.2 %copy.16 = bf16[4,32,8,1024]{3,2,0,1:T(8,128)(2,1)} copy(bf16[4,32,8,1024]{3,2,1,0:T(8,128)(2,1)} %bitcast.18) | data formatting | bytes 4194304 | tf_op jit(solution)/shard_map/all_to_all | solution.py:241
  240.6 0.0 collective-permute-done.6
  240.6 0.0 collective-permute-done.8
  240.6 0.0 collective-permute-done.7
  240.6 0.0 copy-done.3
  240.6 1.8 fusion.37
  (7 shorter events, 0.0 us)
Async XLA Ops:
  7.2 2.6 %copy-start = (bf16[256,1024]{1,0:T(8,128)(2,1)S(1)}, bf16[256,1024]{1,0:T(8,128)(2,1)}, u32[]{:S(2)}) copy-start(bf16[256,1024]{1,0:T(8,128)(2,1)} %param.8) | copy-start | bytes 1572868
  7.2 113.8 %all-gather.2.cloned.1.call-start = ((), (), s32[]{:S(2)}) async-start(), calls=%async_computation.3 | async-start | bytes 4325376 | tf_op jit(solution)/shard_map/all_gather | solution.py:232
  7.9 9.3 %collective-permute-start = (bf16[64,1024]{1,0:T(8,128)(2,1)}, bf16[64,1024]{1,0:T(8,128)(2,1)S(1)}, u32[]{:S(2)}, u32[]{:S(2)}) collective-permute-start(bf16[64,1024]{1,0:T(8,128)(2,1)} %param.10), channel_id=1, source_target_pairs={{0,1},{1,2},{2,3},{3,4},{4,5},{5,6},{6,7},{7,8},{8,9},{9,10},{10,1... | collective-permute-start | bytes 393224 | tf_op jit(solution)/shard_map/ppermute | solution.py:16
  11.2 8.6 %collective-permute-start.2 = (bf16[64,1024]{1,0:T(8,128)(2,1)S(1)}, bf16[64,1024]{1,0:T(8,128)(2,1)S(1)}, u32[]{:S(2)}, u32[]{:S(2)}) collective-permute-start(bf16[64,1024]{1,0:T(8,128)(2,1)S(1)} %fusion.12), channel_id=1, source_target_pairs={{0,1},{1,2},{2,3},{3,4},{4,5},{5,6},{6,7},{7,8},{8,9},{9,10},{10,1... | collective-permute-start | bytes 393224 | tf_op jit(solution)/shard_map/ppermute | solution.py:16
  17.2 8.0 %collective-permute-start.1 = (bf16[64,1024]{1,0:T(8,128)(2,1)S(1)}, bf16[64,1024]{1,0:T(8,128)(2,1)S(1)}, u32[]{:S(2)}, u32[]{:S(2)}) collective-permute-start(bf16[64,1024]{1,0:T(8,128)(2,1)S(1)} %collective-permute-done), channel_id=1, source_target_pairs={{0,1},{1,2},{2,3},{3,4},{4,5},{5,6},{6,7},{7,8},{8,9},{9,10},{10,1... | collective-permute-start | bytes 393224 | tf_op jit(solution)/shard_map/ppermute | solution.py:16
  20.1 8.1 %collective-permute-start.3 = (bf16[64,1024]{1,0:T(8,128)(2,1)S(1)}, bf16[64,1024]{1,0:T(8,128)(2,1)S(1)}, u32[]{:S(2)}, u32[]{:S(2)}) collective-permute-start(bf16[64,1024]{1,0:T(8,128)(2,1)S(1)} %add_convert_fusion.1), channel_id=1, source_target_pairs={{0,1},{1,2},{2,3},{3,4},{4,5},{5,6},{6,7},{7,8},{8,9},{9,10},{10,1... | collective-permute-start | bytes 393224 | tf_op jit(solution)/shard_map/ppermute | solution.py:16
  28.3 5.4 %collective-permute-start.4 = (bf16[64,1024]{1,0:T(8,128)(2,1)S(1)}, bf16[64,1024]{1,0:T(8,128)(2,1)S(1)}, u32[]{:S(2)}, u32[]{:S(2)}) collective-permute-start(bf16[64,1024]{1,0:T(8,128)(2,1)S(1)} %add_convert_fusion), channel_id=1, source_target_pairs={{0,30},{1,31},{2,0},{3,1},{4,2},{5,3},{6,4},{7,5},{8,6},{9,7},{10,... | collective-permute-start | bytes 393224 | tf_op jit(solution)/shard_map/ppermute | solution.py:16
  33.7 0.7 copy-start.2
  121.0 7.1 %copy-start.5 = (bf16[2048,1024]{1,0:T(8,128)(2,1)S(1)}, bf16[2048,1024]{1,0:T(8,128)(2,1)}, u32[]{:S(2)}) copy-start(bf16[2048,1024]{1,0:T(8,128)(2,1)} %get-tuple-element.7) | copy-start | bytes 12582916
  121.0 7.1 %copy-start.7 = (bf16[1024,1024]{1,0:T(8,128)(2,1)S(1)}, bf16[1024,1024]{1,0:T(8,128)(2,1)}, u32[]{:S(2)}) copy-start(bf16[1024,1024]{1,0:T(8,128)(2,1)} %get-tuple-element.8) | copy-start | bytes 6291460
  128.1 8.8 %copy-start.6 = (bf16[1024,1024]{1,0:T(8,128)(2,1)S(1)}, bf16[1024,1024]{1,0:T(8,128)(2,1)}, u32[]{:S(2)}) copy-start(bf16[1024,1024]{1,0:T(8,128)(2,1)} %get-tuple-element.9) | copy-start | bytes 6291460
  136.9 5.0 %copy-start.8 = (bf16[2048,1024]{1,0:T(8,128)(2,1)}, bf16[2048,1024]{1,0:T(8,128)(2,1)S(1)}, u32[]{:S(2)}) copy-start(bf16[2048,1024]{1,0:T(8,128)(2,1)S(1)} %fusion.6) | copy-start | bytes 12582916
  141.9 7.7 %copy-start.1 = (bf16[2048,1024]{1,0:T(8,128)(2,1)}, bf16[2048,1024]{1,0:T(8,128)(2,1)S(1)}, u32[]{:S(2)}) copy-start(bf16[2048,1024]{1,0:T(8,128)(2,1)S(1)} %convolution_convert_fusion) | copy-start | bytes 12582916
  143.7 9.8 %collective-permute-start.5 = (bf16[4,4,64,1024]{3,2,1,0:T(8,128)(2,1)}, bf16[4,4,64,1024]{3,2,1,0:T(8,128)(2,1)}, u32[]{:S(2)}, u32[]{:S(2)}) collective-permute-start(bf16[4,4,64,1024]{3,2,1,0:T(8,128)(2,1)} %dynamic-slice_bitcast_fusion), channel_id=1, source_target_pairs={{0,1},{1,0},{2,3},{3,2},{4,5},{5,4},{6,7},{7,6},{8,9},{9,8},{10,11... | collective-permute-start | bytes 6291464 | tf_op jit(solution)/shard_map/ppermute | solution.py:186
  149.6 29.4 %all-to-all-start.2 = ((bf16[4,256,1024]{2,1,0:T(8,128)(2,1)}), bf16[4,256,1024]{2,1,0:T(8,128)(2,1)S(1)}, u32[]{:S(2)}, u32[]{:S(2)}) async-start(bf16[4,256,1024]{2,1,0:T(8,128)(2,1)} %bitcast.85), calls=%async_computation.2 | async-start | bytes 4194304 | tf_op jit(solution)/shard_map/all_to_all | solution.py:244
  179.0 29.5 %all-to-all-start = ((bf16[4,4,64,1024]{3,2,1,0:T(8,128)(2,1)}), bf16[4,4,64,1024]{3,2,1,0:T(8,128)(2,1)}, u32[]{:S(2)}, u32[]{:S(2)}) async-start(bf16[4,4,64,1024]{3,2,1,0:T(8,128)(2,1)} %fusion.7), calls=%async_computation | async-start | bytes 4194304 | tf_op jit(solution)/shard_map/all_to_all | solution.py:188
  192.9 20.2 %copy-start.4 = (bf16[64,1024]{1,0:T(8,128)(2,1)S(1)}, bf16[64,1024]{1,0:T(8,128)(2,1)}, u32[]{:S(2)}) copy-start(bf16[64,1024]{1,0:T(8,128)(2,1)} %param.10) | copy-start | bytes 393220
  208.6 28.9 %all-to-all-start.1 = ((bf16[4,256,1024]{2,1,0:T(8,128)(2,1)}), bf16[4,256,1024]{2,1,0:T(8,128)(2,1)}, u32[]{:S(2)}, u32[]{:S(2)}) async-start(bf16[4,256,1024]{2,1,0:T(8,128)(2,1)} %bitcast.82), calls=%async_computation.1 | async-start | bytes 4194304 | tf_op jit(solution)/shard_map/all_to_all | solution.py:241
  217.5 23.1 %collective-permute-start.6 = (bf16[64,1024]{1,0:T(8,128)(2,1)}, bf16[64,1024]{1,0:T(8,128)(2,1)}, u32[]{:S(2)}, u32[]{:S(2)}) collective-permute-start(bf16[64,1024]{1,0:T(8,128)(2,1)} %get-tuple-element.10), channel_id=1, source_target_pairs={{0,2},{1,3},{2,4},{3,5},{4,6},{5,7},{6,0},{7,1},{8,10},{9,11},{10,... | collective-permute-start | bytes 393224 | tf_op jit(solution)/shard_map/ppermute | solution.py:194
  218.1 22.5 %collective-permute-start.8 = (bf16[64,1024]{1,0:T(8,128)(2,1)}, bf16[64,1024]{1,0:T(8,128)(2,1)}, u32[]{:S(2)}, u32[]{:S(2)}) collective-permute-start(bf16[64,1024]{1,0:T(8,128)(2,1)} %get-tuple-element.11), channel_id=1, source_target_pairs={{0,6},{1,7},{2,0},{3,1},{4,2},{5,3},{6,4},{7,5},{8,14},{9,15},{10,... | collective-permute-start | bytes 393224 | tf_op jit(solution)/shard_map/ppermute | solution.py:194
  221.3 19.3 %collective-permute-start.7 = (bf16[64,1024]{1,0:T(8,128)(2,1)}, bf16[64,1024]{1,0:T(8,128)(2,1)}, u32[]{:S(2)}, u32[]{:S(2)}) collective-permute-start(bf16[64,1024]{1,0:T(8,128)(2,1)} %get-tuple-element.12), channel_id=1, source_target_pairs={{0,4},{1,5},{2,6},{3,7},{4,0},{5,1},{6,2},{7,3},{8,12},{9,13},{10,... | collective-permute-start | bytes 393224 | tf_op jit(solution)/shard_map/ppermute | solution.py:194
  223.7 16.9 %copy-start.3 = (bf16[64,1024]{1,0:T(8,128)(2,1)S(1)}, bf16[64,1024]{1,0:T(8,128)(2,1)}, u32[]{:S(2)}) copy-start(bf16[64,1024]{1,0:T(8,128)(2,1)} %copy-done.2) | copy-start | bytes 393220
Sparse Core Ops, SparseCore 0:
  11.0 86.2 all-gather.1

commit v3 on v2

--- a/solution.py
+++ b/solution.py
@@ -36,8 +36,8 @@
     )
 
 
-def spread_kernel(n_blk, n_hid, rows_ref, win_ref, wout_ref, all_ref, fin_ref, fout_ref,
-                  keep_in, keep_out, local_sem, w_send, w_recv,
+def spread_kernel(n_blk, n_hid, rows_ref, wout_ref, all_ref, fout_ref,
+                  keep_out, local_sem, w_send, w_recv,
                   a_send, a_recv, b_send, b_recv, c_send, c_recv):
     blk = lax.axis_index("blk")
     hid = lax.axis_index("hid")
@@ -45,8 +45,8 @@
     core = lax.rem(hid, 2)
     place = lax.div(hid, 2)
     cap = rows_ref.shape[0]
-    depth = win_ref.shape[0]
-    width = fin_ref.shape[1]
+    depth = wout_ref.shape[0]
+    width = fout_ref.shape[1]
     mesh_id = pl.DeviceIdType.MESH
 
     def peer_blk(step):
@@ -94,7 +94,6 @@
     locals_ = [pltpu.make_async_copy(rows_ref, all_ref.at[own], local_sem.at[0])]
     mine = pl.ds(pl.multiple_of(blk * width, width), width)
     takes = [
-        pltpu.make_async_copy(win_ref.at[:, mine], keep_in, local_sem.at[1]),
         pltpu.make_async_copy(wout_ref.at[:, mine], keep_out, local_sem.at[2]),
     ]
     for copy in locals_ + takes:
@@ -117,11 +116,9 @@
                                        b_recv.at[far - 1, step], (peer_blk(far), hid))
         twin.append(send(all_ref.at[got], all_ref.at[got], c_send.at[0, step],
                          c_recv.at[0, step], partner))
-    send_weight(0, win_ref, fin_ref)
-    send_weight(1, wout_ref, fout_ref)
+    send_weight(0, wout_ref, fout_ref)
     puts = [
-        pltpu.make_async_copy(keep_in, fin_ref.at[band, :], local_sem.at[3]),
-        pltpu.make_async_copy(keep_out, fout_ref.at[band, :], local_sem.at[4]),
+        pltpu.make_async_copy(keep_out, fout_ref.at[band, :], local_sem.at[1]),
     ]
     for take, put in zip(takes, puts):
         take.wait()
@@ -141,41 +138,38 @@
         copy.wait()
 
 
-def spread(rows, w_in, w_out):
+def spread(rows, w_out):
     n_blk, n_hid = lax.axis_size("blk"), lax.axis_size("hid")
-    depth, hidden = w_in.shape
+    depth, hidden = w_out.shape
     width = hidden // n_blk
     pairs = n_hid // 2
     dma = pltpu.SemaphoreType.DMA
     near = max(pairs - 1, 1)
-    full = jax.ShapeDtypeStruct((depth * n_blk, width), w_in.dtype)
+    full = jax.ShapeDtypeStruct((depth * n_blk, width), w_out.dtype)
     return pl.pallas_call(
         functools.partial(spread_kernel, n_blk, n_hid),
         out_shape=(
             jax.ShapeDtypeStruct((rows.shape[0] * n_blk * n_hid, rows.shape[1]), rows.dtype),
             full,
-            full,
         ),
         in_specs=[
             pl.BlockSpec(memory_space=pltpu.VMEM),
             pl.BlockSpec(memory_space=pl.ANY),
-            pl.BlockSpec(memory_space=pl.ANY),
         ],
-        out_specs=[pl.BlockSpec(memory_space=pl.ANY)] * 3,
+        out_specs=[pl.BlockSpec(memory_space=pl.ANY)] * 2,
         scratch_shapes=[
-            pltpu.VMEM((depth, width), w_in.dtype),
-            pltpu.VMEM((depth, width), w_in.dtype),
-            dma((5,)),
-            dma((2, n_blk - 1)), dma((2, n_blk - 1)),
+            pltpu.VMEM((depth, width), w_out.dtype),
+            dma((3,)),
+            dma((1, n_blk - 1)), dma((1, n_blk - 1)),
             dma((near,)), dma((near,)),
             dma((n_blk - 1, pairs)), dma((n_blk - 1, pairs)),
             dma((n_blk, pairs)), dma((n_blk, pairs)),
         ],
         compiler_params=pltpu.CompilerParams(collective_id=0, has_side_effects=True),
-    )(rows, w_in, w_out)
-
-
-def fold_rows(part):
+    )(rows, w_out)
+
+
+def fold_rows(part, ahead, behind):
     n_blk, n_hid = lax.axis_size("blk"), lax.axis_size("hid")
     pairs = n_hid // 2
     hid = lax.axis_index("hid")
@@ -185,17 +179,19 @@
     keep = lax.dynamic_index_in_dim(parts, core, 2, keepdims=False)
     came = lax.ppermute(give, "hid", [(i, i ^ 1) for i in range(n_hid)])
     both = (keep.astype(jnp.float32) + came.astype(jnp.float32)).astype(part.dtype)
+    both, ahead = lax.optimization_barrier((both, ahead))
     spread_out = lax.all_to_all(both, "blk", 0, 0, tiled=True)
+    spread_out, behind = lax.optimization_barrier((spread_out, behind))
     mine = jnp.sum(spread_out.astype(jnp.float32), axis=0).astype(part.dtype)
     total = lax.dynamic_index_in_dim(mine, place, 0, keepdims=False).astype(jnp.float32)
     for step in range(1, pairs):
         piece = lax.dynamic_index_in_dim(mine, (place + step) % pairs, 0, keepdims=False)
         moves = [(i, (i + 2 * step) % n_hid) for i in range(n_hid)]
         total = total + lax.ppermute(piece, "hid", moves).astype(jnp.float32)
-    return total
-
-
-def shards(images, caption_ids, captions, caption_feats, w_in, w_out, logit_scale, logit_bias):
+    return total, ahead, behind
+
+
+def work(images, caption_ids, captions, caption_feats, w_in, w_out, logit_scale, logit_bias):
     temper = logit_scale[0]
     offset = logit_bias[0]
     cap_rows = captions.shape[0]
@@ -230,27 +226,27 @@
     caption_round = own_grad.astype(jnp.bfloat16)
     both = ("blk", "hid")
     feats_all = lax.all_gather(caption_feats, both, axis=0, tiled=True)
-    rows_all, full_in, full_out = spread(caption_round, w_in, w_out)
+    full_in = lax.all_to_all(w_in, "blk", 1, 0, tiled=True)
+    rows_all, full_out = spread(caption_round, w_out)
     pre_act = jnp.dot(feats_all, full_in, preferred_element_type=jnp.float32)
-    act_grad = jnp.dot(rows_all, full_out, preferred_element_type=jnp.float32)
-    output, gelu_slope = gelu_parts(pre_act)
+    output = gelu_parts(pre_act)[0]
     active = output.astype(jnp.bfloat16)
-    pre_grad = (act_grad * gelu_slope).astype(jnp.bfloat16)
+    out_part = contract(rows_all, active, 0, 0).astype(jnp.bfloat16)
+    out_part, rows_later, pre_later = lax.optimization_barrier((out_part, rows_all, pre_act))
+    w_out_grad = lax.all_to_all(out_part, "blk", 0, 1, tiled=True)
+    act_grad = jnp.dot(rows_later, full_out, preferred_element_type=jnp.float32)
+    pre_grad = (act_grad * gelu_parts(pre_later)[1]).astype(jnp.bfloat16)
+    in_part = contract(feats_all, pre_grad, 0, 0).astype(jnp.bfloat16)
     part = contract(pre_grad, full_in, 1, 1).astype(jnp.bfloat16)
-    branch = fold_rows(part)
-    w_in_grad = lax.all_to_all(
-        contract(feats_all, pre_grad, 0, 0).astype(jnp.bfloat16), "blk", 0, 1, tiled=True
-    )
-    w_out_grad = lax.all_to_all(
-        contract(rows_all, active, 0, 0).astype(jnp.bfloat16), "blk", 0, 1, tiled=True
-    )
+    branch, w_out_grad, in_part = fold_rows(part, w_out_grad, in_part)
+    w_in_grad = lax.all_to_all(in_part, "blk", 0, 1, tiled=True)
     feat_grad = (own_grad + branch).astype(jnp.bfloat16)
     return (image_grad, feat_grad, w_in_grad, w_out_grad)
 
 
 def solution(mesh):
     return jax.shard_map(
-        shards,
+        work,
         mesh=mesh,
         in_specs=(
             P(("blk", "hid"), None),

time: 250 us -> 246 us (0.984)
  Pallas kernels: 86.6 us -> 62.9 us
  local copies, waits for them, and re-layouts: 7.9 us -> 20.3 us
  waiting for transfers between devices: 66.7 us -> 75.1 us
    pallas_call x1, Pallas kernels: 86.6 us -> 62.9 us  [spread(): pl.pallas_call(functools.partial(spread_kernel, n_blk, n_hid), out_shape=...]
    unnamed x18 -> x28, local copies, waits for them, and re-layouts: 0.69 us -> 11 us
    ppermute x3, waiting for transfers between devices: 0.01 us -> 5.56 us  [fold_rows(): total = total + lax.ppermute(piece, 'hid', moves).astype(jnp.float32)]
    all_to_all x2 -> x3, starting transfers between devices: 8.24 us -> 11.9 us  [the longest x1 4.72 us: work(): full_in = lax.all_to_all(w_in, 'blk', 1, 0, tiled=True)]
    all_to_all x2 -> x3, local copies, waits for them, and re-layouts: 4.72 us -> 7.78 us  [the longest x1 3.84 us: work(): w_in_grad = lax.all_to_all(in_part, 'blk', 0, 1, tiled=True)]
    ppermute x5, waiting for transfers between devices: 17.1 us -> 20.1 us  [from_behind(): lax.ppermute(shard, axis, [(i, (i + by) % length) for i in range(length)])]
    all_to_all x2 -> x3, waiting for transfers between devices: 33.2 us -> 33.5 us  [the longest x1 25.8 us: work(): w_out_grad = lax.all_to_all(out_part, 'blk', 0, 1, tiled=True)]
  transfers between devices with their start and end apart: 13 -> 14, of which waited for: 8 -> 9; matrix products, arithmetic and copies ran while one was open for 14% -> 11% of each run, Pallas kernels for 35% -> 26%
where the time goes in v3:
time: 246 us; the launch traced here: 245 us
  waiting for transfers between devices  75.1 us (31%)
  Pallas kernels  62.9 us (26%)
  matrix products  41.9 us (17%)
  starting transfers between devices  22.4 us (9%)
  local copies, waits for them, and re-layouts  20.3 us (8%)
  between operations  15.7 us (6%)
  other arithmetic  6.74 us (3%)
    pallas_call x1, Pallas kernels, spread(): pl.pallas_call(functools.partial(spread_kernel, n_blk, n_hid), out_shape=...  62.9 us
    all_to_all x1, waiting for transfers between devices, work(): w_out_grad = lax.all_to_all(out_part, 'blk', 0, 1, tiled=True)  25.8 us
    dot_general x9, matrix products, contract(): lax.dot_general(left_side, right_side, (((left_dim,), (right_dim,)), ((),...  25.4 us
    ppermute x5, waiting for transfers between devices, from_behind(): lax.ppermute(shard, axis, [(i, (i + by) % length) for i in range(length)])  20.1 us
    all_to_all x1, waiting for transfers between devices, fold_rows(): spread_out = lax.all_to_all(both, 'blk', 0, 0, tiled=True)  15.3 us
    unnamed x28, local copies, waits for them, and re-layouts  11 us
    dot_general x1, matrix products, work(): act_grad = jnp.dot(rows_later, full_out, preferred_element_type=jnp.float32)  8.88 us
    all_to_all x1, waiting for transfers between devices, work(): w_in_grad = lax.all_to_all(in_part, 'blk', 0, 1, tiled=True)  7.7 us
  transfers between devices with their start and end apart: 14, of which 9 were waited for; matrix products, arithmetic and copies ran while one was open for 11% of the time, Pallas kernels for 26%

profile of v3, /device:TPU:0, one launch (start us, length us, event | category | flops | bytes accessed | tf_op | source)
XLA Modules:
  0.0 245.0 jit_solution(12436362556075585388)
XLA Ops:
  7.2 0.0 copy-start
  7.2 0.0 all-gather.2.cloned.1.call-start
  7.2 0.7 all-gather.2.cloned.1.call-update
  7.9 0.0 copy-start.8
  7.9 0.0 copy-start.11
  7.9 0.5 collective-permute-start
  8.5 4.1 %copy.20 = bf16[256,4096]{0,1:T(8,128)(2,1)} copy(bf16[256,4096]{1,0:T(8,128)(2,1)} %param.12) | data formatting | bytes 4194304 | tf_op args[4]
  12.5 4.7 %all-to-all-start = ((bf16[256,4,1024]{0,2,1:T(8,128)(2,1)}), bf16[256,4,1024]{0,2,1:T(8,128)(2,1)S(1)}, u32[]{:S(2)}, u32[]{:S(2)}) async-start(bf16[256,4,1024]{0,2,1:T(8,128)(2,1)} %bitcast.71), calls=%async_computation | async-start | bytes 4194304 | tf_op jit(solution)/shard_map/all_to_all | solution.py:229
  18.6 0.0 copy-done
  18.6 0.0 copy-done.8
  18.6 0.0 copy-done.11
  18.6 0.3 fusion.39
  18.9 0.2 fusion.20
  19.1 1.6 collective-permute-start.2
  20.8 0.0 collective-permute-done
  20.8 0.2 collective-permute-start.1
  21.0 0.3 fusion.40
  21.3 7.1 %collective-permute-done.2 = bf16[64,1024]{1,0:T(8,128)(2,1)S(1)} collective-permute-done((bf16[64,1024]{1,0:T(8,128)(2,1)S(1)}, bf16[64,1024]{1,0:T(8,128)(2,1)S(1)}, u32[]{:S(2)}, u32[]{:S(2)}) %collective-permute-start.2) | collective-permute-done | bytes 131104 | tf_op jit(solution)/shard_map/ppermute | solution.py:16
  28.4 0.2 add_convert_fusion.1
  28.6 0.1 collective-permute-start.3
  28.6 1.9 collective-permute-done.1
  30.6 0.3 fusion.41
  30.9 0.2 convolution_multiply_fusion
  31.1 6.0 %collective-permute-done.3 = bf16[64,1024]{1,0:T(8,128)(2,1)S(1)} collective-permute-done((bf16[64,1024]{1,0:T(8,128)(2,1)S(1)}, bf16[64,1024]{1,0:T(8,128)(2,1)S(1)}, u32[]{:S(2)}, u32[]{:S(2)}) %collective-permute-start.3) | collective-permute-done | bytes 131104 | tf_op jit(solution)/shard_map/ppermute | solution.py:16
  37.2 0.1 collective-permute-start.4
  37.2 5.0 %collective-permute-done.4.rows_ref = bf16[64,1024]{1,0:T(8,128)(2,1)S(1)} collective-permute-done((bf16[64,1024]{1,0:T(8,128)(2,1)S(1)}, bf16[64,1024]{1,0:T(8,128)(2,1)S(1)}, u32[]{:S(2)}, u32[]{:S(2)}) %collective-permute-start.4) | collective-permute-done | bytes 131104 | tf_op jit(solution)/shard_map/ppermute | solution.py:16
  42.2 0.7 copy-done.6
  42.9 62.9 %shard_map.111 = (bf16[2048,1024]{1,0:T(8,128)(2,1)}, bf16[1024,1024]{1,0:T(8,128)(2,1)}) custom-call(bf16[64,1024]{1,0:T(8,128)(2,1)} %copy-done.6, bf16[256,4096]{1,0:T(8,128)(2,1)} %wout_ref.1), custom_call_target="tpu_custom_call" | custom-call | tf_op jit(solution)/shard_map/pallas_call | solution.py:149
  105.8 0.0 all-to-all-done
  105.8 2.4 copy.21
  108.2 7.1 %fusion.51 = f32[2048,1024]{1,0:T(8,128)S(1)} fusion(bf16[2048,1024]{1,0:T(8,128)(2,1)} %all-gather.2.cloned.1.call-done, bf16[1024,1024]{1,0:T(8,128)(2,1)} %bitcast.79), kind=kOutput, calls=%fused_computation.73 | convolution fusion | flops 4294967296 | bytes 14680064 | tf_op jit(solution)/shard_map/dot_general | solution.py:231
  115.2 0.0 copy-done.9
  115.2 6.1 %fusion.15 = bf16[1024,1024]{1,0:T(8,128)(2,1)} fusion(bf16[2048,1024]{1,0:T(8,128)(2,1)S(1)} %copy-done.9, f32[2048,1024]{1,0:T(8,128)S(1)} %fusion.51), kind=kOutput, calls=%fused_computation.22 | convolution fusion | flops 4314890240 | bytes 14680064 | tf_op jit(solution)/shard_map/dot_general | solution.py:31
  121.3 8.9 %fusion.11 = bf16[2048,1024]{1,0:T(8,128)(2,1)S(1)} fusion(f32[2048,1024]{1,0:T(8,128)S(1)} %fusion.51, bf16[2048,1024]{1,0:T(8,128)(2,1)S(1)} %copy-done.9, bf16[1024,1024]{1,0:T(8,128)(2,1)S(1)} %copy-done.10), kind=kOutput, calls=%fused_computation.14 | convolution fusion | flops 4334813184 | bytes 18874368 | tf_op jit(solution)/shard_map/dot_general | solution.py:237
  130.2 5.0 %convolution_convert_fusion = bf16[2048,1024]{1,0:T(8,128)(2,1)S(1)} fusion(bf16[2048,1024]{1,0:T(8,128)(2,1)S(1)} %fusion.11, bf16[1024,1024]{1,0:T(8,128)(2,1)S(1)} %bitcast.80), kind=kOutput, calls=%fused_computation.18 | convolution fusion | flops 4297064448 | bytes 10485760 | tf_op jit(solution)/shard_map/dot_general | solution.py:31
  135.3 2.0 copy-done.3
  137.2 1.5 dynamic-slice_bitcast_fusion
  138.7 0.0 collective-permute-start.5
  138.7 3.6 %all-to-all-start.1 = ((bf16[4,256,1024]{2,1,0:T(8,128)(2,1)}), bf16[4,256,1024]{2,1,0:T(8,128)(2,1)S(1)}, u32[]{:S(2)}, u32[]{:S(2)}) async-start(bf16[4,256,1024]{2,1,0:T(8,128)(2,1)} %bitcast.78), calls=%async_computation.1 | async-start | bytes 4194304 | tf_op jit(solution)/shard_map/all_to_all | solution.py:236
  142.4 25.8 %all-to-all-done.1 = bf16[4,256,1024]{2,1,0:T(8,128)(2,1)S(1)} async-done(((bf16[4,256,1024]{2,1,0:T(8,128)(2,1)}), bf16[4,256,1024]{2,1,0:T(8,128)(2,1)S(1)}, u32[]{:S(2)}, u32[]{:S(2)}) %all-to-all-start.1) | async-done | bytes 2097184 | tf_op jit(solution)/shard_map/all_to_all | solution.py:236
  168.1 1.6 copy.26
  169.7 0.0 collective-permute-done.5
  169.7 1.4 copy-done.4
  171.1 3.9 %fusion.12 = bf16[4,4,64,1024]{3,2,1,0:T(8,128)(2,1)} fusion(bf16[4,4,64,1024]{3,2,1,0:T(8,128)(2,1)} %collective-permute-done.5, bf16[4,4,2,64,1024]{4,3,2,1,0:T(8,128)(2,1)S(1)} %bitcast.76, s32[]{:T(128)S(6)} %select_n.59), kind=kLoop, calls=%fused_computation.16 | loop fusion | flops 4194304 | bytes 6291460 | tf_op jit(solution)/shard_map/convert_element_type | solution.py:181
  175.0 3.8 %all-to-all-start.2 = ((bf16[4,4,64,1024]{3,2,1,0:T(8,128)(2,1)}), bf16[4,4,64,1024]{3,2,1,0:T(8,128)(2,1)S(1)}, u32[]{:S(2)}, u32[]{:S(2)}) async-start(bf16[4,4,64,1024]{3,2,1,0:T(8,128)(2,1)} %fusion.12), calls=%async_computation.2 | async-start | bytes 4194304 | tf_op jit(solution)/shard_map/all_to_all | solution.py:183
  178.8 9.4 %convert_bitcast_fusion = bf16[1024,1024]{0,1:T(8,128)(2,1)} fusion(bf16[2048,1024]{1,0:T(8,128)(2,1)} %copy-done.12, bf16[2048,1024]{1,0:T(8,128)(2,1)} %all-gather.2.cloned.1.call-done), kind=kOutput, calls=%fused_computation.20 | convolution fusion | flops 4296015872 | bytes 10485760 | tf_op jit(solution)/shard_map/dot_general | solution.py:31
  188.2 15.3 %all-to-all-done.2 = bf16[4,4,64,1024]{3,2,1,0:T(8,128)(2,1)S(1)} async-done(((bf16[4,4,64,1024]{3,2,1,0:T(8,128)(2,1)}), bf16[4,4,64,1024]{3,2,1,0:T(8,128)(2,1)S(1)}, u32[]{:S(2)}, u32[]{:S(2)}) %all-to-all-start.2) | async-done | bytes 2097184 | tf_op jit(solution)/shard_map/all_to_all | solution.py:183
  203.5 3.8 %copy.28 = bf16[128,4,8,256]{3,2,0,1:T(8,128)(2,1)} copy(bf16[128,4,8,256]{3,2,1,0:T(8,128)(2,1)} %bitcast.81) | data formatting | bytes 4194304 | tf_op jit(solution)/shard_map/all_to_all | solution.py:242
  207.4 3.6 %all-to-all-start.3 = ((bf16[4,256,1024]{1,2,0:T(8,128)(2,1)}), bf16[4,256,1024]{1,2,0:T(8,128)(2,1)S(1)}, u32[]{:S(2)}, u32[]{:S(2)}) async-start(bf16[4,256,1024]{1,2,0:T(8,128)(2,1)} %bitcast.73), calls=%async_computation.3 | async-start | bytes 4194304 | tf_op jit(solution)/shard_map/all_to_all | solution.py:242
  211.1 0.0 copy-start.7
  211.1 0.3 fusion.50
  211.4 1.3 convolution_add_fusion.1
  212.7 2.1 reduce_sum.12
  214.8 0.4 collective-permute-start.6
  215.2 2.7 %collective-permute-start.7 = (bf16[64,1024]{1,0:T(8,128)(2,1)S(1)}, bf16[64,1024]{1,0:T(8,128)(2,1)S(1)}, u32[]{:S(2)}, u32[]{:S(2)}) collective-permute-start(bf16[64,1024]{1,0:T(8,128)(2,1)S(1)} %get-tuple-element.28), channel_id=1, source_target_pairs={{0,4},{1,5},{2,6},{3,7},{4,0},{5,1},{6,2},{7,3},{8,12},{9,13},{10,... | collective-permute-start | bytes 393224 | tf_op jit(solution)/shard_map/ppermute | solution.py:190
  217.9 1.1 collective-permute-start.8
  219.0 2.3 fusion.19
  221.3 1.7 collective-permute-done.6
  223.0 3.8 %collective-permute-done.7 = bf16[64,1024]{1,0:T(8,128)(2,1)S(1)} collective-permute-done((bf16[64,1024]{1,0:T(8,128)(2,1)S(1)}, bf16[64,1024]{1,0:T(8,128)(2,1)S(1)}, u32[]{:S(2)}, u32[]{:S(2)}) %collective-permute-start.7) | collective-permute-done | bytes 131104 | tf_op jit(solution)/shard_map/ppermute | solution.py:190
  226.9 0.0 collective-permute-done.8
  226.9 0.7 fusion.45
  227.6 7.7 %all-to-all-done.3 = bf16[4,256,1024]{1,2,0:T(8,128)(2,1)S(1)} async-done(((bf16[4,256,1024]{1,2,0:T(8,128)(2,1)}), bf16[4,256,1024]{1,2,0:T(8,128)(2,1)S(1)}, u32[]{:S(2)}, u32[]{:S(2)}) %all-to-all-start.3) | async-done | bytes 2097184 | tf_op jit(solution)/shard_map/all_to_all | solution.py:242
  235.3 2.8 %copy.24 = bf16[256,4096]{1,0:T(8,128)(2,1)} copy(bf16[256,4096]{0,1:T(8,128)(2,1)S(1)} %bitcast.72) | data formatting | bytes 4194304
  238.2 0.0 copy-done.1
  (20 shorter events, 0.1 us)
Async XLA Ops:
  7.2 11.4 %copy-start = (bf16[256,1024]{1,0:T(8,128)(2,1)S(1)}, bf16[256,1024]{1,0:T(8,128)(2,1)}, u32[]{:S(2)}) copy-start(bf16[256,1024]{1,0:T(8,128)(2,1)} %param.8) | copy-start | bytes 1572868
  7.2 101.0 %all-gather.2.cloned.1.call-start = ((), (), s32[]{:S(2)}) async-start(), calls=%async_computation.4 | async-start | bytes 4325376 | tf_op jit(solution)/shard_map/all_gather | solution.py:228
  7.9 10.7 %copy-start.8 = (bf16[64,1024]{1,0:T(8,128)(2,1)S(1)}, bf16[64,1024]{1,0:T(8,128)(2,1)}, u32[]{:S(2)}) copy-start(bf16[64,1024]{1,0:T(8,128)(2,1)} %param.10) | copy-start | bytes 393220
  7.9 10.7 %copy-start.11 = (s32[256]{0:T(256)S(1)}, s32[256]{0:T(256)}, u32[]{:S(2)}) copy-start(s32[256]{0:T(256)} %param.9) | copy-start | bytes 3076
  7.9 12.8 %collective-permute-start = (bf16[64,1024]{1,0:T(8,128)(2,1)}, bf16[64,1024]{1,0:T(8,128)(2,1)S(1)}, u32[]{:S(2)}, u32[]{:S(2)}) collective-permute-start(bf16[64,1024]{1,0:T(8,128)(2,1)} %param.10), channel_id=1, source_target_pairs={{0,1},{1,2},{2,3},{3,4},{4,5},{5,6},{6,7},{7,8},{8,9},{9,10},{10,1... | collective-permute-start | bytes 393224 | tf_op jit(solution)/shard_map/ppermute | solution.py:16
  12.5 93.2 %all-to-all-start = ((bf16[256,4,1024]{0,2,1:T(8,128)(2,1)}), bf16[256,4,1024]{0,2,1:T(8,128)(2,1)S(1)}, u32[]{:S(2)}, u32[]{:S(2)}) async-start(bf16[256,4,1024]{0,2,1:T(8,128)(2,1)} %bitcast.71), calls=%async_computation | async-start | bytes 4194304 | tf_op jit(solution)/shard_map/all_to_all | solution.py:229
  19.1 9.2 %collective-permute-start.2 = (bf16[64,1024]{1,0:T(8,128)(2,1)S(1)}, bf16[64,1024]{1,0:T(8,128)(2,1)S(1)}, u32[]{:S(2)}, u32[]{:S(2)}) collective-permute-start(bf16[64,1024]{1,0:T(8,128)(2,1)S(1)} %fusion.20), channel_id=1, source_target_pairs={{0,1},{1,2},{2,3},{3,4},{4,5},{5,6},{6,7},{7,8},{8,9},{9,10},{10,1... | collective-permute-start | bytes 393224 | tf_op jit(solution)/shard_map/ppermute | solution.py:16
  20.8 9.8 %collective-permute-start.1 = (bf16[64,1024]{1,0:T(8,128)(2,1)S(1)}, bf16[64,1024]{1,0:T(8,128)(2,1)S(1)}, u32[]{:S(2)}, u32[]{:S(2)}) collective-permute-start(bf16[64,1024]{1,0:T(8,128)(2,1)S(1)} %collective-permute-done), channel_id=1, source_target_pairs={{0,1},{1,2},{2,3},{3,4},{4,5},{5,6},{6,7},{7,8},{8,9},{9,10},{10,1... | collective-permute-start | bytes 393224 | tf_op jit(solution)/shard_map/ppermute | solution.py:16
  28.6 8.5 %collective-permute-start.3 = (bf16[64,1024]{1,0:T(8,128)(2,1)S(1)}, bf16[64,1024]{1,0:T(8,128)(2,1)S(1)}, u32[]{:S(2)}, u32[]{:S(2)}) collective-permute-start(bf16[64,1024]{1,0:T(8,128)(2,1)S(1)} %add_convert_fusion.1), channel_id=1, source_target_pairs={{0,1},{1,2},{2,3},{3,4},{4,5},{5,6},{6,7},{7,8},{8,9},{9,10},{10,1... | collective-permute-start | bytes 393224 | tf_op jit(solution)/shard_map/ppermute | solution.py:16
  37.2 5.1 %collective-permute-start.4 = (bf16[64,1024]{1,0:T(8,128)(2,1)S(1)}, bf16[64,1024]{1,0:T(8,128)(2,1)S(1)}, u32[]{:S(2)}, u32[]{:S(2)}) collective-permute-start(bf16[64,1024]{1,0:T(8,128)(2,1)S(1)} %add_convert_fusion), channel_id=1, source_target_pairs={{0,30},{1,31},{2,0},{3,1},{4,2},{5,3},{6,4},{7,5},{8,6},{9,7},{10,... | collective-permute-start | bytes 393224 | tf_op jit(solution)/shard_map/ppermute | solution.py:16
  42.2 0.7 copy-start.6
  108.2 7.1 %copy-start.9 = (bf16[2048,1024]{1,0:T(8,128)(2,1)S(1)}, bf16[2048,1024]{1,0:T(8,128)(2,1)}, u32[]{:S(2)}) copy-start(bf16[2048,1024]{1,0:T(8,128)(2,1)} %get-tuple-element.14) | copy-start | bytes 12582916
  115.2 6.1 %copy-start.10 = (bf16[1024,1024]{1,0:T(8,128)(2,1)S(1)}, bf16[1024,1024]{1,0:T(8,128)(2,1)}, u32[]{:S(2)}) copy-start(bf16[1024,1024]{1,0:T(8,128)(2,1)} %get-tuple-element.15) | copy-start | bytes 6291460
  121.3 8.9 %copy-start.5 = (bf16[4,256,1024]{2,1,0:T(8,128)(2,1)S(1)}, bf16[4,256,1024]{2,1,0:T(8,128)(2,1)}, u32[]{:S(2)}) copy-start(bf16[4,256,1024]{2,1,0:T(8,128)(2,1)} %copy.21) | copy-start | bytes 6291460
  130.2 5.0 %copy-start.12 = (bf16[2048,1024]{1,0:T(8,128)(2,1)}, bf16[2048,1024]{1,0:T(8,128)(2,1)S(1)}, u32[]{:S(2)}) copy-start(bf16[2048,1024]{1,0:T(8,128)(2,1)S(1)} %fusion.11) | copy-start | bytes 12582916
  135.2 2.0 copy-start.3
  138.7 31.0 %collective-permute-start.5 = (bf16[4,4,64,1024]{3,2,1,0:T(8,128)(2,1)}, bf16[4,4,64,1024]{3,2,1,0:T(8,128)(2,1)}, u32[]{:S(2)}, u32[]{:S(2)}) collective-permute-start(bf16[4,4,64,1024]{3,2,1,0:T(8,128)(2,1)} %dynamic-slice_bitcast_fusion), channel_id=1, source_target_pairs={{0,1},{1,0},{2,3},{3,2},{4,5},{5,4},{6,7},{7,6},{8,9},{9,8},{10,11... | collective-permute-start | bytes 6291464 | tf_op jit(solution)/shard_map/ppermute | solution.py:180
  138.7 29.4 %all-to-all-start.1 = ((bf16[4,256,1024]{2,1,0:T(8,128)(2,1)}), bf16[4,256,1024]{2,1,0:T(8,128)(2,1)S(1)}, u32[]{:S(2)}, u32[]{:S(2)}) async-start(bf16[4,256,1024]{2,1,0:T(8,128)(2,1)} %bitcast.78), calls=%async_computation.1 | async-start | bytes 4194304 | tf_op jit(solution)/shard_map/all_to_all | solution.py:236
  168.1 2.9 %copy-start.4 = (bf16[2048,1024]{1,0:T(8,128)(2,1)S(1)}, bf16[2048,1024]{1,0:T(8,128)(2,1)}, u32[]{:S(2)}) copy-start(bf16[2048,1024]{1,0:T(8,128)(2,1)} %copy-done.3) | copy-start | bytes 12582916
  175.0 28.5 %all-to-all-start.2 = ((bf16[4,4,64,1024]{3,2,1,0:T(8,128)(2,1)}), bf16[4,4,64,1024]{3,2,1,0:T(8,128)(2,1)S(1)}, u32[]{:S(2)}, u32[]{:S(2)}) async-start(bf16[4,4,64,1024]{3,2,1,0:T(8,128)(2,1)} %fusion.12), calls=%async_computation.2 | async-start | bytes 4194304 | tf_op jit(solution)/shard_map/all_to_all | solution.py:183
  203.5 3.8 %copy-start.2 = (bf16[4,4,64,1024]{3,2,1,0:T(8,128)(2,1)}, bf16[4,4,64,1024]{3,2,1,0:T(8,128)(2,1)S(1)}, u32[]{:S(2)}) copy-start(bf16[4,4,64,1024]{3,2,1,0:T(8,128)(2,1)S(1)} %all-to-all-done.2) | copy-start | bytes 6291460
  207.4 28.0 %all-to-all-start.3 = ((bf16[4,256,1024]{1,2,0:T(8,128)(2,1)}), bf16[4,256,1024]{1,2,0:T(8,128)(2,1)S(1)}, u32[]{:S(2)}, u32[]{:S(2)}) async-start(bf16[4,256,1024]{1,2,0:T(8,128)(2,1)} %bitcast.73), calls=%async_computation.3 | async-start | bytes 4194304 | tf_op jit(solution)/shard_map/all_to_all | solution.py:242
  211.1 15.8 %copy-start.7 = (bf16[64,1024]{1,0:T(8,128)(2,1)S(1)}, bf16[64,1024]{1,0:T(8,128)(2,1)}, u32[]{:S(2)}) copy-start(bf16[64,1024]{1,0:T(8,128)(2,1)} %copy-done.6) | copy-start | bytes 393220
  212.7 25.5 %copy-start.1 = (bf16[256,1024]{1,0:T(8,128)(2,1)S(1)}, bf16[256,1024]{1,0:T(8,128)(2,1)}, u32[]{:S(2)}) copy-start(bf16[256,1024]{1,0:T(8,128)(2,1)} %param.8) | copy-start | bytes 1572868
  214.8 8.2 %collective-permute-start.6 = (bf16[64,1024]{1,0:T(8,128)(2,1)S(1)}, bf16[64,1024]{1,0:T(8,128)(2,1)S(1)}, u32[]{:S(2)}, u32[]{:S(2)}) collective-permute-start(bf16[64,1024]{1,0:T(8,128)(2,1)S(1)} %get-tuple-element.26), channel_id=1, source_target_pairs={{0,2},{1,3},{2,4},{3,5},{4,6},{5,7},{6,0},{7,1},{8,10},{9,11},{10,... | collective-permute-start | bytes 393224 | tf_op jit(solution)/shard_map/ppermute | solution.py:190
  215.2 11.7 %collective-permute-start.7 = (bf16[64,1024]{1,0:T(8,128)(2,1)S(1)}, bf16[64,1024]{1,0:T(8,128)(2,1)S(1)}, u32[]{:S(2)}, u32[]{:S(2)}) collective-permute-start(bf16[64,1024]{1,0:T(8,128)(2,1)S(1)} %get-tuple-element.28), channel_id=1, source_target_pairs={{0,4},{1,5},{2,6},{3,7},{4,0},{5,1},{6,2},{7,3},{8,12},{9,13},{10,... | collective-permute-start | bytes 393224 | tf_op jit(solution)/shard_map/ppermute | solution.py:190
  217.9 9.0 %collective-permute-start.8 = (bf16[64,1024]{1,0:T(8,128)(2,1)S(1)}, bf16[64,1024]{1,0:T(8,128)(2,1)S(1)}, u32[]{:S(2)}, u32[]{:S(2)}) collective-permute-start(bf16[64,1024]{1,0:T(8,128)(2,1)S(1)} %get-tuple-element.27), channel_id=1, source_target_pairs={{0,6},{1,7},{2,0},{3,1},{4,2},{5,3},{6,4},{7,5},{8,14},{9,15},{10,... | collective-permute-start | bytes 393224 | tf_op jit(solution)/shard_map/ppermute | solution.py:190
Sparse Core Ops, SparseCore 0:
  11.0 94.2 all-gather.1

commit v4 on v3

--- a/solution.py
+++ b/solution.py
@@ -6,6 +6,7 @@
 from jax import lax
 from jax.experimental import pallas as pl
 from jax.experimental.pallas import tpu as pltpu
+from jax.experimental.layout import Layout, with_layout_constraint
 from jax.sharding import PartitionSpec as P
 
 HOPS = 2
@@ -226,7 +227,10 @@
     caption_round = own_grad.astype(jnp.bfloat16)
     both = ("blk", "hid")
     feats_all = lax.all_gather(caption_feats, both, axis=0, tiled=True)
-    full_in = lax.all_to_all(w_in, "blk", 1, 0, tiled=True)
+    n_blk = lax.axis_size("blk")
+    cut = w_in.reshape(w_in.shape[0], n_blk, -1).transpose(1, 0, 2)
+    cut = with_layout_constraint(cut, Layout((0, 1, 2)))
+    full_in = lax.all_to_all(cut, "blk", 0, 0, tiled=True).reshape(-1, cut.shape[2])
     rows_all, full_out = spread(caption_round, w_out)
     pre_act = jnp.dot(feats_all, full_in, preferred_element_type=jnp.float32)
     output = gelu_parts(pre_act)[0]
@@ -237,6 +241,7 @@
     act_grad = jnp.dot(rows_later, full_out, preferred_element_type=jnp.float32)
     pre_grad = (act_grad * gelu_parts(pre_later)[1]).astype(jnp.bfloat16)
     in_part = contract(feats_all, pre_grad, 0, 0).astype(jnp.bfloat16)
+    in_part = with_layout_constraint(in_part, Layout((0, 1)))
     part = contract(pre_grad, full_in, 1, 1).astype(jnp.bfloat16)
     branch, w_out_grad, in_part = fold_rows(part, w_out_grad, in_part)
     w_in_grad = lax.all_to_all(in_part, "blk", 0, 1, tiled=True)

time: 246 us -> 240 us (0.976)
  local copies, waits for them, and re-layouts: 20.3 us -> 15.7 us
    unnamed x28 -> x23, local copies, waits for them, and re-layouts: 11 us -> 8.65 us
  transfers between devices with their start and end apart: 14 -> 14, of which waited for: 9 -> 8; matrix products, arithmetic and copies ran while one was open for 11% -> 10% of each run, Pallas kernels for 26% -> 26%
where the time goes in v4:
time: 240 us
  waiting for transfers between devices  73.6 us (31%)
  Pallas kernels  62.3 us (26%)
  matrix products  41.2 us (17%)
  starting transfers between devices  24.6 us (10%)
  local copies, waits for them, and re-layouts  15.7 us (7%)
  between operations  15.7 us (7%)
  other arithmetic  6.68 us (3%)
    pallas_call x1, Pallas kernels, spread(): pl.pallas_call(functools.partial(spread_kernel, n_blk, n_hid), out_shape=...  62.3 us
    all_to_all x1, waiting for transfers between devices, work(): w_out_grad = lax.all_to_all(out_part, 'blk', 0, 1, tiled=True)  25.8 us
    dot_general x9, matrix products, contract(): lax.dot_general(left_side, right_side, (((left_dim,), (right_dim,)), ((),...  25.2 us
    ppermute x5, waiting for transfers between devices, from_behind(): lax.ppermute(shard, axis, [(i, (i + by) % length) for i in range(length)])  20.5 us
    all_to_all x1, waiting for transfers between devices, fold_rows(): spread_out = lax.all_to_all(both, 'blk', 0, 0, tiled=True)  15.3 us
    dot_general x1, matrix products, work(): act_grad = jnp.dot(rows_later, full_out, preferred_element_type=jnp.float32)  8.89 us
    unnamed x23, local copies, waits for them, and re-layouts  8.65 us
    all_to_all x1, waiting for transfers between devices, work(): w_in_grad = lax.all_to_all(in_part, 'blk', 0, 1, tiled=True)  7.27 us
  transfers between devices with their start and end apart: 14, of which 8 were waited for; matrix products, arithmetic and copies ran while one was open for 10% of the time, Pallas kernels for 26%

profile of v4, /device:TPU:0, one launch (start us, length us, event | category | flops | bytes accessed | tf_op | source)
XLA Modules:
  0.0 239.7 jit_solution(17800108483579310091)
XLA Ops:
  7.2 0.0 copy-start
  7.2 0.0 all-gather.2.cloned.1.call-start
  7.2 0.7 all-gather.2.cloned.1.call-update
  7.9 0.5 collective-permute-start
  8.5 3.3 %copy.14 = bf16[256,4096]{0,1:T(8,128)(2,1)S(1)} copy(bf16[256,4096]{1,0:T(8,128)(2,1)} %param.12) | data formatting | bytes 4194304 | tf_op args[4]
  11.7 0.0 copy-start.6
  11.7 0.0 copy-start.9
  11.8 2.4 copy.15
  14.1 4.7 %all-to-all-start = ((bf16[4,256,1024]{2,1,0:T(8,128)(2,1)}), bf16[4,256,1024]{2,1,0:T(8,128)(2,1)S(1)}, u32[]{:S(2)}, u32[]{:S(2)}) async-start(bf16[4,256,1024]{2,1,0:T(8,128)(2,1)} %bitcast.3), calls=%async_computation | async-start | bytes 4194304 | tf_op jit(solution)/shard_map/all_to_all | solution.py:233
  20.2 0.3 fusion.39
  20.5 0.2 fusion.20
  20.7 1.6 collective-permute-start.2
  22.4 0.0 collective-permute-done
  22.4 0.2 collective-permute-start.1
  22.5 0.3 fusion.40
  22.9 7.9 %collective-permute-done.2 = bf16[64,1024]{1,0:T(8,128)(2,1)S(1)} collective-permute-done((bf16[64,1024]{1,0:T(8,128)(2,1)S(1)}, bf16[64,1024]{1,0:T(8,128)(2,1)S(1)}, u32[]{:S(2)}, u32[]{:S(2)}) %collective-permute-start.2) | collective-permute-done | bytes 131104 | tf_op jit(solution)/shard_map/ppermute | solution.py:17
  30.8 0.2 add_convert_fusion.1
  31.0 0.1 collective-permute-start.3
  31.1 2.0 collective-permute-done.1
  33.0 0.3 fusion.41
  33.3 0.2 convolution_multiply_fusion
  33.6 5.6 %collective-permute-done.3 = bf16[64,1024]{1,0:T(8,128)(2,1)S(1)} collective-permute-done((bf16[64,1024]{1,0:T(8,128)(2,1)S(1)}, bf16[64,1024]{1,0:T(8,128)(2,1)S(1)}, u32[]{:S(2)}, u32[]{:S(2)}) %collective-permute-start.3) | collective-permute-done | bytes 131104 | tf_op jit(solution)/shard_map/ppermute | solution.py:17
  39.2 0.2 collective-permute-start.4
  39.4 5.0 %collective-permute-done.4.rows_ref = bf16[64,1024]{1,0:T(8,128)(2,1)S(1)} collective-permute-done((bf16[64,1024]{1,0:T(8,128)(2,1)S(1)}, bf16[64,1024]{1,0:T(8,128)(2,1)S(1)}, u32[]{:S(2)}, u32[]{:S(2)}) %collective-permute-start.4) | collective-permute-done | bytes 131104 | tf_op jit(solution)/shard_map/ppermute | solution.py:17
  44.4 0.7 copy-done.4
  45.1 62.3 %shard_map.111 = (bf16[2048,1024]{1,0:T(8,128)(2,1)}, bf16[1024,1024]{1,0:T(8,128)(2,1)}) custom-call(bf16[64,1024]{1,0:T(8,128)(2,1)} %copy-done.4, bf16[256,4096]{1,0:T(8,128)(2,1)} %wout_ref.1), custom_call_target="tpu_custom_call" | custom-call | tf_op jit(solution)/shard_map/pallas_call | solution.py:150
  107.4 0.0 all-to-all-done
  107.4 0.0 all-gather.2.cloned.1.call-done
  107.4 6.4 %fusion.51 = f32[2048,1024]{1,0:T(8,128)S(1)} fusion(bf16[2048,1024]{1,0:T(8,128)(2,1)} %all-gather.2.cloned.1.call-done, bf16[1024,1024]{1,0:T(8,128)(2,1)S(1)} %bitcast.73), kind=kOutput, calls=%fused_computation.72 | convolution fusion | flops 4294967296 | bytes 14680064 | tf_op jit(solution)/shard_map/dot_general | solution.py:235
  113.8 0.0 copy-done.7
  113.8 0.0 copy-start.8
  113.9 6.0 %fusion.15 = bf16[1024,1024]{1,0:T(8,128)(2,1)} fusion(bf16[2048,1024]{1,0:T(8,128)(2,1)S(1)} %copy-done.7, f32[2048,1024]{1,0:T(8,128)S(1)} %fusion.51), kind=kOutput, calls=%fused_computation.21 | convolution fusion | flops 4314890240 | bytes 14680064 | tf_op jit(solution)/shard_map/dot_general | solution.py:32
  119.8 0.0 copy-done.8
  119.8 8.9 %fusion.11 = bf16[2048,1024]{1,0:T(8,128)(2,1)S(1)} fusion(f32[2048,1024]{1,0:T(8,128)S(1)} %fusion.51, bf16[2048,1024]{1,0:T(8,128)(2,1)S(1)} %copy-done.7, bf16[1024,1024]{1,0:T(8,128)(2,1)S(1)} %copy-done.8), kind=kOutput, calls=%fused_computation.14 | convolution fusion | flops 4334813184 | bytes 18874368 | tf_op jit(solution)/shard_map/dot_general | solution.py:241
  128.7 5.0 %convolution_convert_fusion = bf16[2048,1024]{1,0:T(8,128)(2,1)S(1)} fusion(bf16[2048,1024]{1,0:T(8,128)(2,1)S(1)} %fusion.11, bf16[1024,1024]{1,0:T(8,128)(2,1)S(1)} %bitcast.74), kind=kOutput, calls=%fused_computation.18 | convolution fusion | flops 4297064448 | bytes 10485760 | tf_op jit(solution)/shard_map/dot_general | solution.py:32
  133.8 2.0 copy-done.2
  135.7 1.5 dynamic-slice_bitcast_fusion
  137.2 0.0 collective-permute-start.5
  137.2 3.6 %all-to-all-start.1 = ((bf16[4,256,1024]{2,1,0:T(8,128)(2,1)}), bf16[4,256,1024]{2,1,0:T(8,128)(2,1)S(1)}, u32[]{:S(2)}, u32[]{:S(2)}) async-start(bf16[4,256,1024]{2,1,0:T(8,128)(2,1)} %bitcast.76), calls=%async_computation.1 | async-start | bytes 4194304 | tf_op jit(solution)/shard_map/all_to_all | solution.py:240
  140.9 25.8 %all-to-all-done.1 = bf16[4,256,1024]{2,1,0:T(8,128)(2,1)S(1)} async-done(((bf16[4,256,1024]{2,1,0:T(8,128)(2,1)}), bf16[4,256,1024]{2,1,0:T(8,128)(2,1)S(1)}, u32[]{:S(2)}, u32[]{:S(2)}) %all-to-all-start.1) | async-done | bytes 2097184 | tf_op jit(solution)/shard_map/all_to_all | solution.py:240
  166.6 1.6 copy.18
  168.2 0.0 collective-permute-done.5
  168.2 1.4 copy-done.3
  169.6 3.9 %fusion.12 = bf16[4,4,64,1024]{3,2,1,0:T(8,128)(2,1)} fusion(bf16[4,4,64,1024]{3,2,1,0:T(8,128)(2,1)} %collective-permute-done.5, bf16[4,4,2,64,1024]{4,3,2,1,0:T(8,128)(2,1)S(1)} %bitcast.71, s32[]{:T(128)S(6)} %select_n.59), kind=kLoop, calls=%fused_computation.16 | loop fusion | flops 4194304 | bytes 6291460 | tf_op jit(solution)/shard_map/convert_element_type | solution.py:182
  173.5 3.8 %all-to-all-start.2 = ((bf16[4,4,64,1024]{3,2,1,0:T(8,128)(2,1)}), bf16[4,4,64,1024]{3,2,1,0:T(8,128)(2,1)S(1)}, u32[]{:S(2)}, u32[]{:S(2)}) async-start(bf16[4,4,64,1024]{3,2,1,0:T(8,128)(2,1)} %fusion.12), calls=%async_computation.2 | async-start | bytes 4194304 | tf_op jit(solution)/shard_map/all_to_all | solution.py:184
  177.3 9.4 %convert_bitcast_fusion = bf16[1024,1024]{1,0:T(8,128)(2,1)} fusion(bf16[2048,1024]{1,0:T(8,128)(2,1)} %copy-done.10, bf16[2048,1024]{1,0:T(8,128)(2,1)} %all-gather.2.cloned.1.call-done), kind=kOutput, calls=%fused_computation.19 | convolution fusion | flops 4296015872 | bytes 10485760 | tf_op jit(solution)/shard_map/dot_general | solution.py:32
  186.7 15.3 %all-to-all-done.2 = bf16[4,4,64,1024]{3,2,1,0:T(8,128)(2,1)S(1)} async-done(((bf16[4,4,64,1024]{3,2,1,0:T(8,128)(2,1)}), bf16[4,4,64,1024]{3,2,1,0:T(8,128)(2,1)S(1)}, u32[]{:S(2)}, u32[]{:S(2)}) %all-to-all-start.2) | async-done | bytes 2097184 | tf_op jit(solution)/shard_map/all_to_all | solution.py:184
  202.0 1.3 copy-done.1
  203.3 3.6 %all-to-all-start.3 = ((bf16[4,256,1024]{2,1,0:T(8,128)(2,1)}), bf16[4,256,1024]{2,1,0:T(8,128)(2,1)S(1)}, u32[]{:S(2)}, u32[]{:S(2)}) async-start(bf16[4,256,1024]{2,1,0:T(8,128)(2,1)} %bitcast.75), calls=%async_computation.3 | async-start | bytes 4194304 | tf_op jit(solution)/shard_map/all_to_all | solution.py:247
  207.0 0.0 copy-start.5
  207.0 0.3 fusion.50
  207.3 1.3 convolution_add_fusion.1
  208.7 2.0 reduce_sum.12
  210.7 3.1 %collective-permute-start.6 = (bf16[64,1024]{1,0:T(8,128)(2,1)S(1)}, bf16[64,1024]{1,0:T(8,128)(2,1)S(1)}, u32[]{:S(2)}, u32[]{:S(2)}) collective-permute-start(bf16[64,1024]{1,0:T(8,128)(2,1)S(1)} %get-tuple-element.22), channel_id=1, source_target_pairs={{0,2},{1,3},{2,4},{3,5},{4,6},{5,7},{6,0},{7,1},{8,10},{9,11},{10,... | collective-permute-start | bytes 393224 | tf_op jit(solution)/shard_map/ppermute | solution.py:191
  213.8 0.2 collective-permute-start.7
  214.0 2.8 %collective-permute-start.8 = (bf16[64,1024]{1,0:T(8,128)(2,1)S(1)}, bf16[64,1024]{1,0:T(8,128)(2,1)S(1)}, u32[]{:S(2)}, u32[]{:S(2)}) collective-permute-start(bf16[64,1024]{1,0:T(8,128)(2,1)S(1)} %get-tuple-element.23), channel_id=1, source_target_pairs={{0,6},{1,7},{2,0},{3,1},{4,2},{5,3},{6,4},{7,5},{8,14},{9,15},{10,... | collective-permute-start | bytes 393224 | tf_op jit(solution)/shard_map/ppermute | solution.py:191
  216.9 2.3 fusion.19
  219.2 0.0 collective-permute-done.6
  219.2 4.1 %collective-permute-done.7 = bf16[64,1024]{1,0:T(8,128)(2,1)S(1)} collective-permute-done((bf16[64,1024]{1,0:T(8,128)(2,1)S(1)}, bf16[64,1024]{1,0:T(8,128)(2,1)S(1)}, u32[]{:S(2)}, u32[]{:S(2)}) %collective-permute-start.7) | collective-permute-done | bytes 131104 | tf_op jit(solution)/shard_map/ppermute | solution.py:191
  223.3 0.0 collective-permute-done.8
  223.3 0.0 copy-done.5
  223.3 0.7 fusion.45
  224.0 7.3 %all-to-all-done.3 = bf16[4,256,1024]{2,1,0:T(8,128)(2,1)S(1)} async-done(((bf16[4,256,1024]{2,1,0:T(8,128)(2,1)}), bf16[4,256,1024]{2,1,0:T(8,128)(2,1)S(1)}, u32[]{:S(2)}, u32[]{:S(2)}) %all-to-all-start.3) | async-done | bytes 2097184 | tf_op jit(solution)/shard_map/all_to_all | solution.py:247
  231.3 1.6 copy.19
  (15 shorter events, 0.1 us)
Async XLA Ops:
  7.2 13.0 %copy-start = (bf16[256,1024]{1,0:T(8,128)(2,1)S(1)}, bf16[256,1024]{1,0:T(8,128)(2,1)}, u32[]{:S(2)}) copy-start(bf16[256,1024]{1,0:T(8,128)(2,1)} %param.8) | copy-start | bytes 1572868
  7.2 100.2 %all-gather.2.cloned.1.call-start = ((), (), s32[]{:S(2)}) async-start(), calls=%async_computation.4 | async-start | bytes 4325376 | tf_op jit(solution)/shard_map/all_gather | solution.py:229
  7.9 14.5 %collective-permute-start = (bf16[64,1024]{1,0:T(8,128)(2,1)}, bf16[64,1024]{1,0:T(8,128)(2,1)S(1)}, u32[]{:S(2)}, u32[]{:S(2)}) collective-permute-start(bf16[64,1024]{1,0:T(8,128)(2,1)} %param.10), channel_id=1, source_target_pairs={{0,1},{1,2},{2,3},{3,4},{4,5},{5,6},{6,7},{7,8},{8,9},{9,10},{10,1... | collective-permute-start | bytes 393224 | tf_op jit(solution)/shard_map/ppermute | solution.py:17
  11.7 8.5 %copy-start.6 = (bf16[64,1024]{1,0:T(8,128)(2,1)S(1)}, bf16[64,1024]{1,0:T(8,128)(2,1)}, u32[]{:S(2)}) copy-start(bf16[64,1024]{1,0:T(8,128)(2,1)} %param.10) | copy-start | bytes 393220
  11.7 8.5 %copy-start.9 = (s32[256]{0:T(256)S(1)}, s32[256]{0:T(256)}, u32[]{:S(2)}) copy-start(s32[256]{0:T(256)} %param.9) | copy-start | bytes 3076
  14.1 93.2 %all-to-all-start = ((bf16[4,256,1024]{2,1,0:T(8,128)(2,1)}), bf16[4,256,1024]{2,1,0:T(8,128)(2,1)S(1)}, u32[]{:S(2)}, u32[]{:S(2)}) async-start(bf16[4,256,1024]{2,1,0:T(8,128)(2,1)} %bitcast.3), calls=%async_computation | async-start | bytes 4194304 | tf_op jit(solution)/shard_map/all_to_all | solution.py:233
  20.7 10.0 %collective-permute-start.2 = (bf16[64,1024]{1,0:T(8,128)(2,1)S(1)}, bf16[64,1024]{1,0:T(8,128)(2,1)S(1)}, u32[]{:S(2)}, u32[]{:S(2)}) collective-permute-start(bf16[64,1024]{1,0:T(8,128)(2,1)S(1)} %fusion.20), channel_id=1, source_target_pairs={{0,1},{1,2},{2,3},{3,4},{4,5},{5,6},{6,7},{7,8},{8,9},{9,10},{10,1... | collective-permute-start | bytes 393224 | tf_op jit(solution)/shard_map/ppermute | solution.py:17
  22.4 10.7 %collective-permute-start.1 = (bf16[64,1024]{1,0:T(8,128)(2,1)S(1)}, bf16[64,1024]{1,0:T(8,128)(2,1)S(1)}, u32[]{:S(2)}, u32[]{:S(2)}) collective-permute-start(bf16[64,1024]{1,0:T(8,128)(2,1)S(1)} %collective-permute-done), channel_id=1, source_target_pairs={{0,1},{1,2},{2,3},{3,4},{4,5},{5,6},{6,7},{7,8},{8,9},{9,10},{10,1... | collective-permute-start | bytes 393224 | tf_op jit(solution)/shard_map/ppermute | solution.py:17
  31.0 8.1 %collective-permute-start.3 = (bf16[64,1024]{1,0:T(8,128)(2,1)S(1)}, bf16[64,1024]{1,0:T(8,128)(2,1)S(1)}, u32[]{:S(2)}, u32[]{:S(2)}) collective-permute-start(bf16[64,1024]{1,0:T(8,128)(2,1)S(1)} %add_convert_fusion.1), channel_id=1, source_target_pairs={{0,1},{1,2},{2,3},{3,4},{4,5},{5,6},{6,7},{7,8},{8,9},{9,10},{10,1... | collective-permute-start | bytes 393224 | tf_op jit(solution)/shard_map/ppermute | solution.py:17
  39.2 5.3 %collective-permute-start.4 = (bf16[64,1024]{1,0:T(8,128)(2,1)S(1)}, bf16[64,1024]{1,0:T(8,128)(2,1)S(1)}, u32[]{:S(2)}, u32[]{:S(2)}) collective-permute-start(bf16[64,1024]{1,0:T(8,128)(2,1)S(1)} %add_convert_fusion), channel_id=1, source_target_pairs={{0,30},{1,31},{2,0},{3,1},{4,2},{5,3},{6,4},{7,5},{8,6},{9,7},{10,... | collective-permute-start | bytes 393224 | tf_op jit(solution)/shard_map/ppermute | solution.py:17
  44.4 0.7 copy-start.4
  107.4 6.4 %copy-start.7 = (bf16[2048,1024]{1,0:T(8,128)(2,1)S(1)}, bf16[2048,1024]{1,0:T(8,128)(2,1)}, u32[]{:S(2)}) copy-start(bf16[2048,1024]{1,0:T(8,128)(2,1)} %get-tuple-element.14) | copy-start | bytes 12582916
  113.8 6.0 %copy-start.8 = (bf16[1024,1024]{1,0:T(8,128)(2,1)S(1)}, bf16[1024,1024]{1,0:T(8,128)(2,1)}, u32[]{:S(2)}) copy-start(bf16[1024,1024]{1,0:T(8,128)(2,1)} %get-tuple-element.15) | copy-start | bytes 6291460
  128.7 5.0 %copy-start.10 = (bf16[2048,1024]{1,0:T(8,128)(2,1)}, bf16[2048,1024]{1,0:T(8,128)(2,1)S(1)}, u32[]{:S(2)}) copy-start(bf16[2048,1024]{1,0:T(8,128)(2,1)S(1)} %fusion.11) | copy-start | bytes 12582916
  133.7 2.0 copy-start.2
  137.2 31.0 %collective-permute-start.5 = (bf16[4,4,64,1024]{3,2,1,0:T(8,128)(2,1)}, bf16[4,4,64,1024]{3,2,1,0:T(8,128)(2,1)}, u32[]{:S(2)}, u32[]{:S(2)}) collective-permute-start(bf16[4,4,64,1024]{3,2,1,0:T(8,128)(2,1)} %dynamic-slice_bitcast_fusion), channel_id=1, source_target_pairs={{0,1},{1,0},{2,3},{3,2},{4,5},{5,4},{6,7},{7,6},{8,9},{9,8},{10,11... | collective-permute-start | bytes 6291464 | tf_op jit(solution)/shard_map/ppermute | solution.py:181
  137.2 29.4 %all-to-all-start.1 = ((bf16[4,256,1024]{2,1,0:T(8,128)(2,1)}), bf16[4,256,1024]{2,1,0:T(8,128)(2,1)S(1)}, u32[]{:S(2)}, u32[]{:S(2)}) async-start(bf16[4,256,1024]{2,1,0:T(8,128)(2,1)} %bitcast.76), calls=%async_computation.1 | async-start | bytes 4194304 | tf_op jit(solution)/shard_map/all_to_all | solution.py:240
  166.6 2.9 %copy-start.3 = (bf16[2048,1024]{1,0:T(8,128)(2,1)S(1)}, bf16[2048,1024]{1,0:T(8,128)(2,1)}, u32[]{:S(2)}) copy-start(bf16[2048,1024]{1,0:T(8,128)(2,1)} %copy-done.2) | copy-start | bytes 12582916
  173.5 28.5 %all-to-all-start.2 = ((bf16[4,4,64,1024]{3,2,1,0:T(8,128)(2,1)}), bf16[4,4,64,1024]{3,2,1,0:T(8,128)(2,1)S(1)}, u32[]{:S(2)}, u32[]{:S(2)}) async-start(bf16[4,4,64,1024]{3,2,1,0:T(8,128)(2,1)} %fusion.12), calls=%async_computation.2 | async-start | bytes 4194304 | tf_op jit(solution)/shard_map/all_to_all | solution.py:184
  202.0 1.3 copy-start.1
  203.3 28.0 %all-to-all-start.3 = ((bf16[4,256,1024]{2,1,0:T(8,128)(2,1)}), bf16[4,256,1024]{2,1,0:T(8,128)(2,1)S(1)}, u32[]{:S(2)}, u32[]{:S(2)}) async-start(bf16[4,256,1024]{2,1,0:T(8,128)(2,1)} %bitcast.75), calls=%async_computation.3 | async-start | bytes 4194304 | tf_op jit(solution)/shard_map/all_to_all | solution.py:247
  207.0 16.3 %copy-start.5 = (bf16[64,1024]{1,0:T(8,128)(2,1)S(1)}, bf16[64,1024]{1,0:T(8,128)(2,1)}, u32[]{:S(2)}) copy-start(bf16[64,1024]{1,0:T(8,128)(2,1)} %copy-done.4) | copy-start | bytes 393220
  210.7 8.5 %collective-permute-start.6 = (bf16[64,1024]{1,0:T(8,128)(2,1)S(1)}, bf16[64,1024]{1,0:T(8,128)(2,1)S(1)}, u32[]{:S(2)}, u32[]{:S(2)}) collective-permute-start(bf16[64,1024]{1,0:T(8,128)(2,1)S(1)} %get-tuple-element.22), channel_id=1, source_target_pairs={{0,2},{1,3},{2,4},{3,5},{4,6},{5,7},{6,0},{7,1},{8,10},{9,11},{10,... | collective-permute-start | bytes 393224 | tf_op jit(solution)/shard_map/ppermute | solution.py:191
  213.8 9.5 %collective-permute-start.7 = (bf16[64,1024]{1,0:T(8,128)(2,1)S(1)}, bf16[64,1024]{1,0:T(8,128)(2,1)S(1)}, u32[]{:S(2)}, u32[]{:S(2)}) collective-permute-start(bf16[64,1024]{1,0:T(8,128)(2,1)S(1)} %get-tuple-element.24), channel_id=1, source_target_pairs={{0,4},{1,5},{2,6},{3,7},{4,0},{5,1},{6,2},{7,3},{8,12},{9,13},{10,... | collective-permute-start | bytes 393224 | tf_op jit(solution)/shard_map/ppermute | solution.py:191
  214.0 9.2 %collective-permute-start.8 = (bf16[64,1024]{1,0:T(8,128)(2,1)S(1)}, bf16[64,1024]{1,0:T(8,128)(2,1)S(1)}, u32[]{:S(2)}, u32[]{:S(2)}) collective-permute-start(bf16[64,1024]{1,0:T(8,128)(2,1)S(1)} %get-tuple-element.23), channel_id=1, source_target_pairs={{0,6},{1,7},{2,0},{3,1},{4,2},{5,3},{6,4},{7,5},{8,14},{9,15},{10,... | collective-permute-start | bytes 393224 | tf_op jit(solution)/shard_map/ppermute | solution.py:191
Sparse Core Ops, SparseCore 0:
  11.0 95.9 all-gather.1
